TPU v7x, 128 devices: a whole 4x4x4 slice. The times are simulated.
128 devices in a mesh: gz: 16 (over z_hi, x, core), gy: 8 (over z_lo, y).
Axes of the slice: x: 4, y: 4, z: 4 (z_hi: 2, z_lo: 2; z = z_hi * 2 + z_lo), core: 2. Of those that a mesh axis runs over, the one named last changes fastest.
Arguments:
- gauge_links: float32 [3, 2, 3, 3, 128, 128, 128], P(None, None, None, None, 'gz', 'gy'), may hold values from -22 to 22
Outputs:
- rotated: float32 [3, 2, 3, 3, 128, 128, 128], P(None, None, None, None, 'gz', 'gy')
All inputs are finite; a program needn't handle non-finite values.
Results may differ from a plain program's by a relative error of at most 0.00015.
Values sent between devices are 32-bit elements; how exact they have to be, the bound alone decides.
A program may use at most 64 MiB of HBM per device.

v0:
```python
import functools
import math

import jax
import jax.numpy as jnp
import numpy as np
from jax import lax
from jax.experimental import pallas as pl
from jax.experimental.pallas import tpu as pltpu
from jax.sharding import PartitionSpec as P

L = 128
ALPHA_HALF = 0.04
BZ = 8
BY = 16
NC = 8
NP = BZ + 1
MESH = pl.DeviceIdType.MESH
F32 = jnp.float32
BF16 = jnp.bfloat16
CHUNKS = ((0, 3), (3, 6), (6, 9))


def tables():
    k = np.arange(L)
    angle = 2.0 * np.pi / L * (np.outer(k, k) % L)
    hartley = np.cos(angle) + np.sin(angle)
    high = hartley.astype(np.float32).astype(jnp.bfloat16)
    low = (hartley - high.astype(np.float64)).astype(np.float32).astype(jnp.bfloat16)
    half = np.concatenate([high, low], axis=1)
    mat_x = np.concatenate([half, half], axis=0)
    mat_y = np.ascontiguousarray(mat_x.T)
    momentum = 4.0 * np.sin(np.pi * k / L) ** 2
    mass = momentum[:, None] + momentum[None, :]
    mass[0, 0] = 1.0
    root = np.sqrt(mass * mass / 4.0 + mass)
    decay = 1.0 / (1.0 + mass / 2.0 + root)
    factor = 12.0 * ALPHA_HALF / (L * L) / (2.0 * root)
    decay[0, 0] = 0.0
    factor[0, 0] = 0.0
    return mat_x, mat_y, decay.astype(np.float32), factor.astype(np.float32)


def split(x):
    high = x.astype(BF16)
    low = (x - high.astype(F32)).astype(BF16)
    return high, low


def transform_x(x, mat_x):
    high, low = split(x)
    out = jnp.dot(jnp.concatenate([high, low], axis=1), mat_x, preferred_element_type=F32)
    return out[:, :L] + out[:, L:]


def transform_y(planes, mat_y):
    wide = jnp.concatenate(planes, axis=1)
    high, low = split(wide)
    out = jnp.dot(mat_y, jnp.concatenate([high, low], axis=0), preferred_element_type=F32)
    return out[:L] + out[L:]


def algebra(re, im):
    trace_part = (im(0, 0) + im(1, 1) + im(2, 2)) * (1.0 / 3.0)
    return [
        im(0, 0) - trace_part,
        im(1, 1) - trace_part,
        (re(0, 1) - re(1, 0)) * 0.5,
        (im(0, 1) + im(1, 0)) * 0.5,
        (re(0, 2) - re(2, 0)) * 0.5,
        (im(0, 2) + im(2, 0)) * 0.5,
        (re(1, 2) - re(2, 1)) * 0.5,
        (im(1, 2) + im(2, 1)) * 0.5,
    ]


def smooth_kernel(
    nz,
    ny,
    links,
    mat_x_in,
    mat_y_in,
    decay_in,
    factor_in,
    out_main,
    out_face,
    link,
    send_a,
    face_a,
    recv_a,
    face_r,
    field,
    send_b,
    recv_b,
    send_e,
    recv_e,
    send_c,
    recv_c,
    send_d,
    face_d,
    mat_x,
    mat_y,
    decay,
    factor,
    load_sem,
    own_sem,
    a_send,
    a_recv,
    b_send,
    b_recv,
    c_send,
    c_recv,
    d_send,
    d_recv,
):
    gz = lax.axis_index("gz")
    gy = lax.axis_index("gy")
    lines = L // nz
    extent = nz * BZ
    last = len(CHUNKS)

    barrier = pltpu.get_barrier_semaphore()
    for r in range(1, ny):
        pl.semaphore_signal(
            barrier, inc=1, device_id=(gz, lax.rem(gy + r, ny)), device_id_type=MESH
        )
    for r in range(1, nz):
        pl.semaphore_signal(
            barrier, inc=1, device_id=(lax.rem(gz + r, nz), gy), device_id_type=MESH
        )

    loads = [pltpu.make_async_copy(links.at[1], link.at[1], load_sem.at[0])]
    ranges = [(lo, min(hi, BZ)) for lo, hi in CHUNKS]
    for n, (lo, hi) in enumerate(ranges):
        for m, mu in enumerate((0, 2)):
            loads.append(
                pltpu.make_async_copy(
                    links.at[mu, :, :, :, lo:hi],
                    link.at[mu, :, :, :, lo:hi],
                    load_sem.at[1 + 2 * n + m],
                )
            )
    base = 1 + 2 * len(CHUNKS)
    small = [
        pltpu.make_async_copy(src, dst, load_sem.at[base + n])
        for n, (src, dst) in enumerate(
            ((mat_x_in, mat_x), (mat_y_in, mat_y), (decay_in, decay), (factor_in, factor))
        )
    ]
    for copy in loads:
        copy.start()
    for copy in small:
        copy.start()

    def remote(src, dst, send, recv, device):
        return pltpu.make_async_remote_copy(
            src_ref=src,
            dst_ref=dst,
            send_sem=send,
            recv_sem=recv,
            device_id=device,
            device_id_type=MESH,
        )

    def rows(block):
        return pl.ds(pl.multiple_of(block * BY, BY), BY)

    def tile(block):
        return pl.ds(pl.multiple_of(block * BZ, BZ), BZ)

    def copy_a(n, r, sender):
        lo, hi = CHUNKS[n]
        target = lax.rem(gy + r, ny)
        return remote(
            send_a.at[target, lo:hi],
            recv_a.at[lo:hi, rows(sender)],
            a_send.at[n, r],
            a_recv.at[n, r],
            (gz, target),
        )

    def copy_face_a(r, sender):
        target = lax.rem(gy + r, ny)
        return remote(
            face_a.at[tile(target)],
            face_r.at[tile(sender)],
            a_send.at[last, r],
            a_recv.at[last, r],
            (gz, target),
        )

    row_index = lax.broadcasted_iota(jnp.int32, (BY, L), 0)
    first_row = row_index == 0

    def entries(mu, z):
        def re(i, j):
            return link[mu, 0, i, j, z]

        def im(i, j):
            return link[mu, 1, i, j, z]

        return re, im

    loads[0].wait()

    def part_y(z, carry):
        parts = algebra(*entries(1, z))
        for c in range(NC):
            behind = jnp.where(first_row, 0.0, pltpu.roll(parts[c], 1, 0))
            send_a[c, z] = behind - parts[c]
            face_a[pl.ds(c * BZ + z, 1), :] = parts[c][BY - 1 : BY]
        return carry

    lax.fori_loop(0, BZ, part_y, 0)

    pl.semaphore_wait(barrier, nz + ny - 2)
    for r in range(1, ny):
        copy_face_a(r, gy).start()
    own_face = pltpu.make_async_copy(face_a.at[tile(gy)], face_r.at[tile(gy)], own_sem.at[last])
    own_face.start()

    carry = [jnp.zeros((BY, L), F32) for _ in range(NC)]
    own_a = []
    for n, (lo, hi) in enumerate(ranges):
        loads[1 + 2 * n].wait()
        loads[2 + 2 * n].wait()

        def part_xz(z, below):
            along_x = algebra(*entries(0, z))
            along_z = algebra(*entries(2, z))
            for c in range(NC):
                shifted = pltpu.roll(along_x[c], 1, 1)
                send_a[c, z] += (shifted - along_x[c]) + (below[c] - along_z[c])
            return along_z

        carry = lax.fori_loop(lo, hi, part_xz, carry)
        if CHUNKS[n][1] == NP:
            for c in range(NC):
                send_a[c, BZ] = carry[c]
        for r in range(1, ny):
            copy_a(n, r, gy).start()
        lo, hi = CHUNKS[n]
        own = pltpu.make_async_copy(
            send_a.at[gy, lo:hi], recv_a.at[lo:hi, rows(gy)], own_sem.at[n]
        )
        own.start()
        own_a.append(own)

    for copy in small:
        copy.wait()
    own_face.wait()
    for r in range(1, ny):
        copy_face_a(r, lax.rem(gy + ny - r, ny)).wait_recv()

    for n, (lo, hi) in enumerate(CHUNKS):
        own_a[n].wait()
        for r in range(1, ny):
            copy_a(n, r, lax.rem(gy + ny - r, ny)).wait_recv()
        for z in range(lo, min(hi, BZ)):
            edge = pltpu.roll(face_r[pl.ds(z, ny, stride=BZ), :], 1, 0)
            recv_a[z, pl.ds(0, ny, stride=BY), :] += edge
        data = transform_x(recv_a[lo:hi].reshape((hi - lo) * L, L), mat_x[...])
        data = transform_y([data[i * L : (i + 1) * L] for i in range(hi - lo)], mat_y[...])
        for i in range(hi - lo):
            field[lo + i] = data[:, i * L : (i + 1) * L]

    rate = decay[...]
    up = field[0]
    down = field[BZ]
    for i in range(1, NP):
        up = field[i] + rate * up
        down = field[BZ - i] + rate * down
    send_b[:, 0] = up.reshape(nz, lines, L)
    send_b[:, 1] = down.reshape(nz, lines, L)
    lane = lax.broadcasted_iota(jnp.int32, (1, L), 1)
    packed = jnp.zeros((1, L), F32)
    for i in range(NP):
        packed = jnp.where(lane == i, jnp.sum(jnp.where(lane == 0, field[i, 0:1, :], 0.0)), packed)
    send_e[0] = packed

    def copy_b(r, sender):
        target = lax.rem(gz + r, nz)
        return remote(
            send_b.at[target], recv_b.at[sender], b_send.at[0, r], b_recv.at[0, r], (target, gy)
        )

    def copy_e(r, sender):
        target = lax.rem(gz + r, nz)
        return remote(
            send_e.at[0], recv_e.at[sender], b_send.at[1, r], b_recv.at[1, r], (target, gy)
        )

    def copy_c(r, sender):
        target = lax.rem(gz + r, nz)
        return remote(
            send_c.at[target], recv_c.at[sender], c_send.at[r], c_recv.at[r], (target, gy)
        )

    for r in range(1, nz):
        copy_b(r, gz).start()
    for r in range(1, nz):
        copy_e(r, gz).start()
    recv_b[gz] = send_b[gz]
    recv_e[gz] = packed

    rate8 = decay[pl.ds(pl.multiple_of(gz * lines, lines), lines), :]
    rate8 = rate8 * rate8
    rate8 = rate8 * rate8
    rate8 = rate8 * rate8
    whole = rate8
    for _ in range(int(math.log2(nz))):
        whole = whole * whole
    images = 1.0 / (1.0 - whole)

    for r in range(1, nz):
        copy_b(r, lax.rem(gz + nz - r, nz)).wait_recv()

    up = recv_b[0, 0]
    down = recv_b[nz - 1, 1]
    for j in range(1, nz):
        up = recv_b[j, 0] + rate8 * up
        down = recv_b[nz - 1 - j, 1] + rate8 * down
    up = up * images
    down = down * images
    for j in range(nz):
        send_c[j, 0] = up
        send_c[nz - 1 - j, 1] = down
        if j < nz - 1:
            up = recv_b[j, 0] + rate8 * up
            down = recv_b[nz - 1 - j, 1] + rate8 * down
    for r in range(1, nz):
        copy_c(r, gz).start()
    recv_c[gz] = send_c[gz]

    for r in range(1, nz):
        copy_e(r, lax.rem(gz + nz - r, nz)).wait_recv()
    sources = recv_e[:, 0, :]
    block = lax.broadcasted_iota(jnp.int32, (nz, L), 0)
    plane = lax.broadcasted_iota(jnp.int32, (nz, L), 1)
    corner = (lax.broadcasted_iota(jnp.int32, (8, L), 0) == 0) & (
        lax.broadcasted_iota(jnp.int32, (8, L), 1) == 0
    )
    constant = (1.0 + extent * extent - 1.0) / extent
    zero_line = []
    for i in range(NP):
        gap = BZ * (gz - block) + i - plane
        gap = jnp.where(gap < 0, gap + extent, gap).astype(F32)
        weight = constant - (6.0 / extent) * gap * (extent - gap)
        weight = jnp.where(plane < NP, weight * (ALPHA_HALF / (L * L)), 0.0)
        zero_line.append(jnp.where(corner, jnp.sum(weight * sources), 0.0))

    for r in range(1, nz):
        copy_c(r, lax.rem(gz + nz - r, nz)).wait_recv()

    rate = decay[...]
    scale = factor[...]
    down = recv_c[:, 1].reshape(L, L)
    ahead = [None] * NP
    for i in range(BZ, -1, -1):
        recv_a[i] = down
        if i > 0:
            down = rate * (down + field[i])
    up = field[0] + recv_c[:, 0].reshape(L, L)
    for i in range(NP):
        if i > 0:
            up = field[i] + rate * up
        recv_a[i] = scale * (up + recv_a[i])
        recv_a[i, 0:8, :] += zero_line[i]

    def copy_d(n, r, owner):
        lo, hi = CHUNKS[n]
        target = lax.rem(gy + r, ny)
        return remote(
            send_d.at[lo:hi, rows(target)],
            out_main.at[owner, lo:hi],
            d_send.at[n, r],
            d_recv.at[n, r],
            (gz, target),
        )

    def copy_face_d(r, owner):
        target = lax.rem(gy + r, ny)
        return remote(
            face_d.at[tile(target)],
            out_face.at[tile(owner)],
            d_send.at[last, r],
            d_recv.at[last, r],
            (gz, target),
        )

    own_d = []
    for n, (lo, hi) in enumerate(CHUNKS):
        data = transform_y([recv_a[i] for i in range(lo, hi)], mat_y[...])
        data = jnp.concatenate(
            [data[:, i * L : (i + 1) * L] for i in range(hi - lo)], axis=0
        )
        data = transform_x(data, mat_x[...])
        send_d[lo:hi] = data.reshape(hi - lo, L, L)
        for r in range(1, ny):
            copy_d(n, r, gy).start()
        own = pltpu.make_async_copy(
            send_d.at[lo:hi, rows(gy)], out_main.at[gy, lo:hi], own_sem.at[last + 1 + n]
        )
        own.start()
        own_d.append(own)
        for z in range(lo, min(hi, BZ)):
            edge = send_d[z, pl.ds(0, ny, stride=BY), :]
            face_d[pl.ds(z, ny, stride=BZ), :] = pltpu.roll(edge, ny - 1, 0)
    for r in range(1, ny):
        copy_face_d(r, gy).start()
    own = pltpu.make_async_copy(
        face_d.at[tile(gy)], out_face.at[tile(gy)], own_sem.at[2 * last + 1]
    )
    own.start()
    own_d.append(own)

    for copy in own_d:
        copy.wait()
    for r in range(1, ny):
        sender = lax.rem(gy + ny - r, ny)
        for n in range(last):
            copy_d(n, r, sender).wait_recv()
        copy_face_d(r, sender).wait_recv()
    for r in range(1, ny):
        for n in range(last):
            copy_a(n, r, gy).wait_send()
            copy_d(n, r, gy).wait_send()
        copy_face_a(r, gy).wait_send()
        copy_face_d(r, gy).wait_send()
    for r in range(1, nz):
        copy_b(r, gz).wait_send()
        copy_e(r, gz).wait_send()
        copy_c(r, gz).wait_send()


def smooth(links, nz, ny):
    mat_x, mat_y, decay, factor = tables()
    last = len(CHUNKS)
    lines = L // nz
    vmem = pltpu.VMEM
    dma = pltpu.SemaphoreType.DMA
    anywhere = pl.BlockSpec(memory_space=pl.ANY)
    return pl.pallas_call(
        functools.partial(smooth_kernel, nz, ny),
        out_shape=(
            jax.ShapeDtypeStruct((NC, NP, BY, L), F32),
            jax.ShapeDtypeStruct((NC * BZ, L), F32),
        ),
        in_specs=[anywhere] * 5,
        out_specs=(anywhere, anywhere),
        scratch_shapes=[
            vmem((3, 2, 3, 3, BZ, BY, L), F32),
            vmem((NC, NP, BY, L), F32),
            vmem((NC * BZ, L), F32),
            vmem((NP, L, L), F32),
            vmem((ny * BZ, L), F32),
            vmem((NP, L, L), F32),
            vmem((nz, 2, lines, L), F32),
            vmem((nz, 2, lines, L), F32),
            vmem((1, 1, L), F32),
            vmem((nz, 1, L), F32),
            vmem((nz, 2, lines, L), F32),
            vmem((nz, 2, lines, L), F32),
            vmem((NP, L, L), F32),
            vmem((ny * BZ, L), F32),
            vmem((2 * L, 2 * L), BF16),
            vmem((2 * L, 2 * L), BF16),
            vmem((L, L), F32),
            vmem((L, L), F32),
            dma((5 + 2 * last,)),
            dma((2 * last + 2,)),
            dma((last + 1, ny)),
            dma((last + 1, ny)),
            dma((2, nz)),
            dma((2, nz)),
            dma((nz,)),
            dma((nz,)),
            dma((last + 1, ny)),
            dma((last + 1, ny)),
        ],
        compiler_params=pltpu.CompilerParams(collective_id=0, has_side_effects=True),
        name="smooth",
    )(links, jnp.asarray(mat_x), jnp.asarray(mat_y), jnp.asarray(decay), jnp.asarray(factor))


def exponent(h):
    h2 = -(h[0] + h[1])
    diag = (h[0], h[1], h2)
    re01, im01 = h[3], -h[2]
    re02, im02 = h[5], -h[4]
    re12, im12 = h[7], -h[6]
    n01 = re01 * re01 + im01 * im01
    n02 = re02 * re02 + im02 * im02
    n12 = re12 * re12 + im12 * im12
    s0 = h[0] * h[0] + n01 + n02
    s1 = h[1] * h[1] + n01 + n12
    s2 = h2 * h2 + n02 + n12
    s01re = re02 * re12 + im02 * im12 - h2 * re01
    s01im = im02 * re12 - re02 * im12 - h2 * im01
    s02re = re01 * re12 - im01 * im12 - h[1] * re02
    s02im = re01 * im12 + im01 * re12 - h[1] * im02
    s12re = re01 * re02 + im01 * im02 - h[0] * re12
    s12im = re01 * im02 - im01 * re02 - h[0] * im12
    p = 0.5 * (s0 + s1 + s2)
    cross = (re01 * re12 - im01 * im12) * re02 + (re01 * im12 + im01 * re12) * im02
    d = h[0] * h[1] * h2 + 2.0 * cross - h[0] * n12 - h[1] * n02 - h2 * n01
    pp = p * p
    dd = d * d
    dp = d * p
    cubes = dd + p * pp
    a0 = 1.0 + dd * (p * (2.0 / 40320.0) - 1.0 / 720.0)
    b0 = d * (-1.0 / 6.0 + p * (1.0 / 120.0) - pp * (1.0 / 5040.0))
    a1 = d * (1.0 / 24.0 - p * (2.0 / 720.0) + pp * (3.0 / 40320.0))
    b1 = 1.0 - p * (1.0 / 6.0) + pp * (1.0 / 120.0) - cubes * (1.0 / 5040.0)
    a2 = -0.5 + p * (1.0 / 24.0) - pp * (1.0 / 720.0) + cubes * (1.0 / 40320.0)
    b2 = d * (1.0 / 120.0) - dp * (2.0 / 5040.0)
    re = {}
    im = {}
    for j, s in enumerate((s0, s1, s2)):
        re[j, j] = a0 + a1 * diag[j] + a2 * s
        im[j, j] = b0 + b1 * diag[j] + b2 * s
    for i, j, hr, hi, sr, si in (
        (0, 1, re01, im01, s01re, s01im),
        (0, 2, re02, im02, s02re, s02im),
        (1, 2, re12, im12, s12re, s12im),
    ):
        rr = a1 * hr + a2 * sr
        ii = b1 * hi + b2 * si
        ri = a1 * hi + a2 * si
        ir = b1 * hr + b2 * sr
        re[i, j] = rr - ii
        im[i, j] = ri + ir
        re[j, i] = rr + ii
        im[j, i] = ir - ri
    return [re[i, j] for i in range(3) for j in range(3)] + [
        im[i, j] for i in range(3) for j in range(3)
    ]


def rotate_kernel(link, main, face, out, here, edge):
    z = pl.program_id(0)
    slot = lax.rem(z, 2)
    other = 1 - slot

    def fill(where, plane):
        for s in range(0, BY, 8):
            g = exponent([main[c, plane, s : s + 8] for c in range(NC)])
            for k in range(18):
                here[where, k, s : s + 8] = g[k]

    @pl.when(z == 0)
    def _():
        g = exponent([face[c * BZ : (c + 1) * BZ] for c in range(NC)])
        for k in range(18):
            edge[k] = g[k]
        fill(0, 0)

    fill(other, z + 1)
    for k in range(18):
        here[slot, k, BY : BY + 1] = edge[k, pl.ds(z, 1)]

    for s in range(0, BY, 8):
        g = [here[slot, k, s : s + 8] for k in range(18)]
        for mu in range(3):
            if mu == 0:
                ahead = [pltpu.roll(x, L - 1, 1) for x in g]
            elif mu == 1:
                ahead = [here[slot, k, s + 1 : s + 9] for k in range(18)]
            else:
                ahead = [here[other, k, s : s + 8] for k in range(18)]
            u = [
                link[mu, p, i, j, 0, s : s + 8]
                for p in range(2)
                for i in range(3)
                for j in range(3)
            ]
            for i in range(3):
                left = []
                for k in range(3):
                    re = im = None
                    for j in range(3):
                        ar, ai = g[3 * i + j], g[9 + 3 * i + j]
                        br, bi = u[3 * j + k], u[9 + 3 * j + k]
                        tr = ar * br - ai * bi
                        ti = ar * bi + ai * br
                        re = tr if re is None else re + tr
                        im = ti if im is None else im + ti
                    left.append((re, im))
                for l in range(3):
                    re = im = None
                    for k in range(3):
                        ar, ai = left[k]
                        br, bi = ahead[3 * l + k], ahead[9 + 3 * l + k]
                        tr = ar * br + ai * bi
                        ti = ai * br - ar * bi
                        re = tr if re is None else re + tr
                        im = ti if im is None else im + ti
                    out[mu, 0, i, l, 0, s : s + 8] = re
                    out[mu, 1, i, l, 0, s : s + 8] = im


def rotate(links, main, face):
    block = pl.BlockSpec((3, 2, 3, 3, 1, BY, L), lambda z: (0, 0, 0, 0, z, 0, 0))
    return pl.pallas_call(
        rotate_kernel,
        grid=(BZ,),
        out_shape=jax.ShapeDtypeStruct(links.shape, F32),
        in_specs=[
            block,
            pl.BlockSpec((NC, NP, BY, L), lambda z: (0, 0, 0, 0)),
            pl.BlockSpec((NC * BZ, L), lambda z: (0, 0)),
        ],
        out_specs=block,
        scratch_shapes=[pltpu.VMEM((2, 18, BY + 8, L), F32), pltpu.VMEM((18, BZ, L), F32)],
        compiler_params=pltpu.CompilerParams(dimension_semantics=("arbitrary",)),
        name="rotate",
    )(links, main, face)


def solution(mesh):
    nz, ny = mesh.shape["gz"], mesh.shape["gy"]

    def body(links):
        main, face = smooth(links, nz, ny)
        return rotate(links, main, face)

    spec = P(None, None, None, None, "gz", "gy", None)
    return jax.shard_map(body, mesh=mesh, in_specs=(spec,), out_specs=spec, check_vma=False)
```

profile of v0, /device:TPU:1, one launch (start us, length us, event | category | flops | bytes accessed | tf_op | source)
XLA Modules:
  0.0 48.5 jit_solution(3919908425380691564)
XLA Ops:
  0.0 40.5 %smooth.1 = (f32[8,9,16,128]{3,2,1,0:T(8,128)}, f32[64,128]{1,0:T(8,128)}) custom-call(f32[3,2,3,3,8,16,128]{6,5,4,3,2,1,0:T(8,128)} %link.1, bf16[256,256]{1,0:T(8,128)(2,1)} %constant.8.clone.mat_x_in, bf16[256,256]{1,0:T(8,128)(2,1)} %constant.9.clone.mat_y_in, f32[128,128]{1,0:T(8,128)} %constant.10.clone.decay_in, f32[128,128]{1,0:T(8,128)} %constant.11.clone.factor_in), custom_call_target="tpu_custom_call" | custom-call | tf_op jit(solution)/shard_map/smooth/pallas_call | solution.py:443
  40.5 8.0 %rotate.1 = f32[3,2,3,3,8,16,128]{6,5,4,3,2,1,0:T(8,128)} custom-call(f32[3,2,3,3,8,16,128]{6,5,4,3,2,1,0:T(8,128)} %link.1, f32[8,9,16,128]{3,2,1,0:T(8,128)} %get-tuple-element.7.main, f32[64,128]{1,0:T(8,128)} %get-tuple-element.8.face), custom_call_target="tpu_custom_call" | custom-call | tf_op jit(solution)/shard_map/rotate/pallas_call | solution.py:604
where the time goes:
time: 48.8 us; the launch traced here: 48.5 us
  Pallas kernels  48.5 us (99%)
    pallas_call x1, Pallas kernels, smooth(): pl.pallas_call(functools.partial(smooth_kernel, nz, ny), out_shape=(jax.S...  40.5 us
    pallas_call x1, Pallas kernels, rotate(): pl.pallas_call(rotate_kernel, grid=(BZ,), out_shape=jax.ShapeDtypeStruct(...  8 us

commit v1 on v0

v1 whole, which is shorter than its diff:
```python
import functools
import math

import jax
import jax.numpy as jnp
import numpy as np
from jax import lax
from jax.experimental import pallas as pl
from jax.experimental.pallas import tpu as pltpu
from jax.sharding import PartitionSpec as P

L = 128
ALPHA_HALF = 0.04
BZ = 8
BY = 16
NC = 8
MESH = pl.DeviceIdType.MESH
F32 = jnp.float32
BF16 = jnp.bfloat16
FORTH = ((6, 8), (4, 6), (2, 4), (1, 2), (0, 1))
BACK = ((0, 2), (2, 4), (4, 6), (6, 8))
BACK_EARLY = 2


def tables():
    k = np.arange(L)
    angle = 2.0 * np.pi / L * (np.outer(k, k) % L)
    hartley = np.cos(angle) + np.sin(angle)
    high = hartley.astype(np.float32).astype(jnp.bfloat16)
    low = (hartley - high.astype(np.float64)).astype(np.float32).astype(jnp.bfloat16)
    half = np.concatenate([high, low], axis=1)
    mat_x = np.concatenate([half, half], axis=0)
    mat_y = np.ascontiguousarray(mat_x.T)
    momentum = 4.0 * np.sin(np.pi * k / L) ** 2
    mass = momentum[:, None] + momentum[None, :]
    mass[0, 0] = 1.0
    root = np.sqrt(mass * mass / 4.0 + mass)
    decay = 1.0 / (1.0 + mass / 2.0 + root)
    factor = 12.0 * ALPHA_HALF / (L * L) / (2.0 * root)
    decay[0, 0] = 0.0
    factor[0, 0] = 0.0
    return mat_x, mat_y, decay.astype(np.float32), factor.astype(np.float32)


def split(x):
    high = x.astype(BF16)
    low = (x - high.astype(F32)).astype(BF16)
    return high, low


def transform_x(planes, mat_x):
    high, low = split(jnp.concatenate(planes, axis=0))
    out = jnp.dot(jnp.concatenate([high, low], axis=1), mat_x, preferred_element_type=F32)
    out = out[:, :L] + out[:, L:]
    return [out[i * L : (i + 1) * L] for i in range(len(planes))]


def transform_y(planes, mat_y):
    high, low = split(jnp.concatenate(planes, axis=1))
    out = jnp.dot(mat_y, jnp.concatenate([high, low], axis=0), preferred_element_type=F32)
    out = out[:L] + out[L:]
    return [out[:, i * L : (i + 1) * L] for i in range(len(planes))]


def algebra(re, im):
    trace_part = (im(0, 0) + im(1, 1) + im(2, 2)) * (1.0 / 3.0)
    return [
        im(0, 0) - trace_part,
        im(1, 1) - trace_part,
        (re(0, 1) - re(1, 0)) * 0.5,
        (im(0, 1) + im(1, 0)) * 0.5,
        (re(0, 2) - re(2, 0)) * 0.5,
        (im(0, 2) + im(2, 0)) * 0.5,
        (re(1, 2) - re(2, 1)) * 0.5,
        (im(1, 2) + im(2, 1)) * 0.5,
    ]


def fix_kernel(
    nz,
    ny,
    links,
    mat_x_in,
    mat_y_in,
    decay_in,
    factor_in,
    out,
    link,
    send_a,
    edge_y,
    recv_a,
    edge_r,
    edge_z,
    below_z,
    field,
    send_b,
    recv_b,
    send_e,
    recv_e,
    send_c,
    recv_c,
    send_d,
    edge_d,
    main,
    above_z,
    edge_g,
    mat_x,
    mat_y,
    decay,
    factor,
    turn,
    turn_edge,
    load_sem,
    small_sem,
    own_sem,
    edge_sem,
    a_send,
    a_recv,
    b_send,
    b_recv,
    c_send,
    c_recv,
    d_send,
    d_recv,
    e_send,
    e_recv,
    z_send,
    z_recv,
):
    gz = lax.axis_index("gz")
    gy = lax.axis_index("gy")
    lines = L // nz
    extent = nz * BZ

    barrier = pltpu.get_barrier_semaphore()
    for r in range(1, ny):
        pl.semaphore_signal(
            barrier, inc=1, device_id=(gz, lax.rem(gy + r, ny)), device_id_type=MESH
        )
    for r in range(1, nz):
        pl.semaphore_signal(
            barrier, inc=1, device_id=(lax.rem(gz + r, nz), gy), device_id_type=MESH
        )
    between = lax.rem(gy + ny // 2, ny)
    for r in range(nz):
        pl.semaphore_signal(
            barrier, inc=1, device_id=(lax.rem(gz + r, nz), between), device_id_type=MESH
        )

    def load(mu, z):
        return pltpu.make_async_copy(
            links.at[mu, :, :, :, pl.ds(z, 1)],
            link.at[mu, :, :, :, pl.ds(z, 1)],
            load_sem.at[mu, z],
        )

    small = [
        pltpu.make_async_copy(src, dst, small_sem.at[n])
        for n, (src, dst) in enumerate(
            ((mat_x_in, mat_x), (mat_y_in, mat_y), (decay_in, decay), (factor_in, factor))
        )
    ]
    for z in range(BZ):
        load(1, z).start()
    load(2, BZ - 1).start()
    for z in range(BZ - 1, -1, -1):
        if z > 0:
            load(2, z - 1).start()
        load(0, z).start()
    for copy in small:
        copy.start()

    def remote(src, dst, send, recv, device):
        return pltpu.make_async_remote_copy(
            src_ref=src,
            dst_ref=dst,
            send_sem=send,
            recv_sem=recv,
            device_id=device,
            device_id_type=MESH,
        )

    def rows(block):
        return pl.ds(pl.multiple_of(block * BY, BY), BY)

    def tile(block):
        return pl.ds(pl.multiple_of(block * BZ, BZ), BZ)

    def y_target(r):
        return lax.rem(gy + r, ny)

    def y_sender(r):
        return lax.rem(gy + ny - r, ny)

    def z_target(r):
        return lax.rem(gz + r, nz)

    def z_sender(r):
        return lax.rem(gz + nz - r, nz)

    def copy_a(n, r, sender):
        lo, hi = FORTH[n]
        return remote(
            send_a.at[y_target(r), lo:hi],
            recv_a.at[lo:hi, rows(sender)],
            a_send.at[n, r],
            a_recv.at[n, r],
            (gz, y_target(r)),
        )

    def own_a(n):
        lo, hi = FORTH[n]
        return pltpu.make_async_copy(
            send_a.at[gy, lo:hi], recv_a.at[lo:hi, rows(gy)], own_sem.at[0, n]
        )

    def copy_edge_a(r, sender):
        return remote(
            edge_y.at[tile(y_target(r))],
            edge_r.at[tile(sender)],
            e_send.at[0, r],
            e_recv.at[0, r],
            (gz, y_target(r)),
        )

    copy_up = remote(edge_z, below_z, z_send.at[0], z_recv.at[0], (z_target(1), gy))
    copy_down = remote(
        main.at[:, 0], above_z, z_send.at[1], z_recv.at[1], (z_target(nz - 1), gy)
    )

    first_row = lax.broadcasted_iota(jnp.int32, (BY, L), 0) == 0

    def parts(mu, z):
        return algebra(
            lambda i, j: link[mu, 0, i, j, z], lambda i, j: link[mu, 1, i, j, z]
        )

    def part_y(z, carry):
        load(1, z).wait()
        along = parts(1, z)
        for c in range(NC):
            behind = jnp.where(first_row, 0.0, pltpu.roll(along[c], 1, 0))
            send_a[c, z] = behind - along[c]
            edge_y[pl.ds(c * BZ + z, 1), :] = along[c][BY - 1 : BY]
        return carry

    lax.fori_loop(0, BZ, part_y, 0)
    load(2, BZ - 1).wait()
    top = parts(2, BZ - 1)
    for c in range(NC):
        edge_z[c] = top[c]

    pl.semaphore_wait(barrier, 2 * nz + ny - 2)
    copy_up.start()
    for r in range(1, ny):
        copy_edge_a(r, gy).start()
    own_edge_a = pltpu.make_async_copy(edge_y.at[tile(gy)], edge_r.at[tile(gy)], edge_sem.at[0])
    own_edge_a.start()

    def gather(z, under, here):
        along = parts(0, z)
        for c in range(NC):
            shifted = pltpu.roll(along[c], 1, 1)
            send_a[c, z] += (shifted - along[c]) + (under[c] - here[c])

    def start_a(n):
        for r in range(1, ny):
            copy_a(n, r, gy).start()
        own_a(n).start()

    def step(t, here):
        z = BZ - 1 - t
        load(2, z - 1).wait()
        load(0, z).wait()
        under = parts(2, z - 1)
        gather(z, under, here)
        return under

    def receive(n):
        own_a(n).wait()
        for r in range(1, ny):
            copy_a(n, r, y_sender(r)).wait_recv()
        lo, hi = FORTH[n]
        for z in range(lo, hi):
            edge = pltpu.roll(edge_r[pl.ds(z, ny, stride=BZ), :], 1, 0)
            recv_a[z, pl.ds(0, ny, stride=BY), :] += edge
        data = transform_x([recv_a[z] for z in range(lo, hi)], mat_x[...])
        data = transform_y(data, mat_y[...])
        for z in range(lo, hi):
            field[z] = data[z - lo]

    bottom = top
    for n, (lo, hi) in enumerate(FORTH):
        if lo > 0:
            bottom = lax.fori_loop(BZ - hi, BZ - lo, step, bottom)
            start_a(n)
    load(0, 0).wait()
    copy_up.wait_recv()
    gather(0, [below_z[c] for c in range(NC)], bottom)
    start_a(len(FORTH) - 1)

    for copy in small:
        copy.wait()
    own_edge_a.wait()
    for r in range(1, ny):
        copy_edge_a(r, y_sender(r)).wait_recv()
    for n in range(len(FORTH)):
        receive(n)

    rate = decay[...]
    up = field[0]
    down = field[BZ - 1]
    for i in range(1, BZ):
        up = field[i] + rate * up
        down = field[BZ - 1 - i] + rate * down
    send_b[:, 0] = (rate * up).reshape(nz, lines, L)
    send_b[:, 1] = down.reshape(nz, lines, L)

    def copy_b(r, sender):
        return remote(
            send_b.at[z_target(r)],
            recv_b.at[sender],
            b_send.at[0, r],
            b_recv.at[0, r],
            (z_target(r), between),
        )

    def copy_e(r, sender):
        return remote(
            send_e.at[0],
            recv_e.at[sender],
            b_send.at[1, r],
            b_recv.at[1, r],
            (z_target(r), gy),
        )

    def copy_c(r, sender):
        return remote(
            send_c.at[z_target(r)],
            recv_c.at[sender],
            c_send.at[r],
            c_recv.at[r],
            (z_target(r), between),
        )

    for r in range(nz):
        copy_b(r, gz).start()
    lane = lax.broadcasted_iota(jnp.int32, (1, L), 1)
    packed = jnp.zeros((1, L), F32)
    for i in range(BZ):
        packed = jnp.where(lane == i, jnp.sum(jnp.where(lane == 0, field[i, 0:1, :], 0.0)), packed)
    send_e[0] = packed
    for r in range(1, nz):
        copy_e(r, gz).start()
    recv_e[gz] = packed

    rate8 = decay[pl.ds(pl.multiple_of(gz * lines, lines), lines), :]
    rate8 = rate8 * rate8
    rate8 = rate8 * rate8
    rate8 = rate8 * rate8
    whole = rate8
    for _ in range(int(math.log2(nz))):
        whole = whole * whole
    images = 1.0 / (1.0 - whole)

    for r in range(nz):
        copy_b(r, z_sender(r)).wait_recv()

    up = recv_b[0, 0]
    down = recv_b[nz - 1, 1]
    for j in range(1, nz):
        up = recv_b[j, 0] + rate8 * up
        down = recv_b[nz - 1 - j, 1] + rate8 * down
    up = up * images
    down = down * images
    for j in range(nz):
        send_c[j, 0] = up
        send_c[nz - 1 - j, 1] = down
        if j < nz - 1:
            up = recv_b[j, 0] + rate8 * up
            down = recv_b[nz - 1 - j, 1] + rate8 * down
    for r in range(nz):
        copy_c(r, gz).start()

    for r in range(1, nz):
        copy_e(r, z_sender(r)).wait_recv()
    sources = recv_e[:, 0, :]
    block = lax.broadcasted_iota(jnp.int32, (nz, L), 0)
    plane = lax.broadcasted_iota(jnp.int32, (nz, L), 1)
    corner = (lax.broadcasted_iota(jnp.int32, (8, L), 0) == 0) & (
        lax.broadcasted_iota(jnp.int32, (8, L), 1) == 0
    )
    constant = (1.0 + extent * extent - 1.0) / extent
    zero_line = []
    for i in range(BZ):
        gap = BZ * (gz - block) + i - plane
        gap = jnp.where(gap < 0, gap + extent, gap).astype(F32)
        weight = constant - (6.0 / extent) * gap * (extent - gap)
        weight = jnp.where(plane < BZ, weight * (ALPHA_HALF / (L * L)), 0.0)
        zero_line.append(jnp.where(corner, jnp.sum(weight * sources), 0.0))

    for r in range(nz):
        copy_c(r, z_sender(r)).wait_recv()

    rate = decay[...]
    scale = factor[...]
    down = rate * recv_c[:, 1].reshape(L, L)
    for i in range(BZ - 1, -1, -1):
        recv_a[i] = down
        if i > 0:
            down = rate * (down + field[i])
    up = recv_c[:, 0].reshape(L, L)
    for i in range(BZ):
        up = field[i] + (rate * up if i > 0 else up)
        recv_a[i] = scale * (up + recv_a[i])
        recv_a[i, 0:8, :] += zero_line[i]

    def copy_d(n, r, owner):
        lo, hi = BACK[n]
        return remote(
            send_d.at[lo:hi, rows(y_target(r))],
            main.at[owner, lo:hi],
            d_send.at[n, r],
            d_recv.at[n, r],
            (gz, y_target(r)),
        )

    def own_d(n):
        lo, hi = BACK[n]
        return pltpu.make_async_copy(
            send_d.at[lo:hi, rows(gy)], main.at[gy, lo:hi], own_sem.at[1, n]
        )

    def copy_edge_d(r, owner):
        return remote(
            edge_d.at[tile(y_target(r))],
            edge_g.at[tile(owner)],
            e_send.at[1, r],
            e_recv.at[1, r],
            (gz, y_target(r)),
        )

    own_edge_d = pltpu.make_async_copy(edge_d.at[tile(gy)], edge_g.at[tile(gy)], edge_sem.at[1])

    def start_d(n):
        for r in range(1, ny):
            copy_d(n, r, gy).start()
        own_d(n).start()

    for n, (lo, hi) in enumerate(BACK):
        data = transform_y([recv_a[z] for z in range(lo, hi)], mat_y[...])
        data = transform_x(data, mat_x[...])
        for z in range(lo, hi):
            send_d[z] = data[z - lo]
            edge = send_d[z, pl.ds(0, ny, stride=BY), :]
            edge_d[pl.ds(z, ny, stride=BZ), :] = pltpu.roll(edge, ny - 1, 0)
        if n < BACK_EARLY:
            start_d(n)
    for r in range(1, ny):
        copy_edge_d(r, gy).start()
    own_edge_d.start()
    for n in range(BACK_EARLY, len(BACK)):
        start_d(n)

    def fill(plane, value):
        for s in range(0, BY, 8):
            g = exponent([value(c, s) for c in range(NC)])
            for k in range(18):
                turn[plane, k, s : s + 8] = g[k]

    def rotate(z, directions, halves=(0, 8)):
        for s in halves:
            g = [turn[z, k, s : s + 8] for k in range(18)]
            for mu in directions:
                if mu == 0:
                    ahead = [pltpu.roll(x, L - 1, 1) for x in g]
                elif mu == 1:
                    ahead = [turn[z, k, s + 1 : s + 9] for k in range(18)]
                else:
                    ahead = [turn[z + 1, k, s : s + 8] for k in range(18)]
                rotate_link(link, out, mu, z, s, g, ahead)

    def arrive(n):
        own_d(n).wait()
        for r in range(1, ny):
            copy_d(n, r, y_sender(r)).wait_recv()

    def plane_step(z, carry):
        fill(z, lambda c, s: main[c, z, s : s + 8])
        rotate(z, (0,))
        rotate(z, (1,), (0,))
        rotate(z - 1, (2,))
        return carry

    def edge_step(z, carry):
        for k in range(18):
            turn[z, k, BY : BY + 1] = turn_edge[k, pl.ds(z, 1)]
        rotate(z, (1,), (8,))
        return carry

    for n, (lo, hi) in enumerate(BACK):
        arrive(n)
        if n == 0:
            copy_down.start()
            fill(0, lambda c, s: main[c, 0, s : s + 8])
            rotate(0, (0,))
            rotate(0, (1,), (0,))
        lax.fori_loop(max(lo, 1), hi, plane_step, 0)
    own_edge_d.wait()
    for r in range(1, ny):
        copy_edge_d(r, y_sender(r)).wait_recv()
    g = exponent([edge_g[c * BZ : (c + 1) * BZ] for c in range(NC)])
    for k in range(18):
        turn_edge[k] = g[k]
    lax.fori_loop(0, BZ, edge_step, 0)
    copy_down.wait_recv()
    fill(BZ, lambda c, s: above_z[c, s : s + 8])
    rotate(BZ - 1, (2,))

    for r in range(1, ny):
        for n in range(len(FORTH)):
            copy_a(n, r, gy).wait_send()
        for n in range(len(BACK)):
            copy_d(n, r, gy).wait_send()
        copy_edge_a(r, gy).wait_send()
        copy_edge_d(r, gy).wait_send()
    for r in range(nz):
        copy_b(r, gz).wait_send()
        copy_c(r, gz).wait_send()
    for r in range(1, nz):
        copy_e(r, gz).wait_send()
    copy_up.wait_send()
    copy_down.wait_send()


def rotate_link(link, out, mu, z, s, g, ahead):
    u = [link[mu, p, i, j, z, s : s + 8] for p in range(2) for i in range(3) for j in range(3)]
    for i in range(3):
        left = []
        for k in range(3):
            re = im = None
            for j in range(3):
                ar, ai = g[3 * i + j], g[9 + 3 * i + j]
                br, bi = u[3 * j + k], u[9 + 3 * j + k]
                tr = ar * br - ai * bi
                ti = ar * bi + ai * br
                re = tr if re is None else re + tr
                im = ti if im is None else im + ti
            left.append((re, im))
        for l in range(3):
            re = im = None
            for k in range(3):
                ar, ai = left[k]
                br, bi = ahead[3 * l + k], ahead[9 + 3 * l + k]
                tr = ar * br + ai * bi
                ti = ai * br - ar * bi
                re = tr if re is None else re + tr
                im = ti if im is None else im + ti
            out[mu, 0, i, l, z, s : s + 8] = re
            out[mu, 1, i, l, z, s : s + 8] = im


def fix(links, nz, ny):
    mat_x, mat_y, decay, factor = tables()
    lines = L // nz
    vmem = pltpu.VMEM
    dma = pltpu.SemaphoreType.DMA
    return pl.pallas_call(
        functools.partial(fix_kernel, nz, ny),
        out_shape=pltpu.VMEM(links.shape, F32),
        in_specs=[pl.BlockSpec(memory_space=pltpu.HBM)] * 5,
        out_specs=pl.BlockSpec(memory_space=pltpu.VMEM),
        scratch_shapes=[
            vmem((3, 2, 3, 3, BZ, BY, L), F32),
            vmem((NC, BZ, BY, L), F32),
            vmem((NC * BZ, L), F32),
            vmem((BZ, L, L), F32),
            vmem((ny * BZ, L), F32),
            vmem((NC, BY, L), F32),
            vmem((NC, BY, L), F32),
            vmem((BZ, L, L), F32),
            vmem((nz, 2, lines, L), F32),
            vmem((nz, 2, lines, L), F32),
            vmem((1, 1, L), F32),
            vmem((nz, 1, L), F32),
            vmem((nz, 2, lines, L), F32),
            vmem((nz, 2, lines, L), F32),
            vmem((BZ, L, L), F32),
            vmem((ny * BZ, L), F32),
            vmem((NC, BZ, BY, L), F32),
            vmem((NC, BY, L), F32),
            vmem((NC * BZ, L), F32),
            vmem((2 * L, 2 * L), BF16),
            vmem((2 * L, 2 * L), BF16),
            vmem((L, L), F32),
            vmem((L, L), F32),
            vmem((BZ + 1, 18, BY + 8, L), F32),
            vmem((18, BZ, L), F32),
            dma((3, BZ)),
            dma((4,)),
            dma((2, BZ)),
            dma((2,)),
            dma((BZ, ny)),
            dma((BZ, ny)),
            dma((2, nz)),
            dma((2, nz)),
            dma((nz,)),
            dma((nz,)),
            dma((BZ, ny)),
            dma((BZ, ny)),
            dma((2, ny)),
            dma((2, ny)),
            dma((2,)),
            dma((2,)),
        ],
        compiler_params=pltpu.CompilerParams(
            collective_id=0, has_side_effects=True, vmem_limit_bytes=32 << 20
        ),
        name="fix",
    )(*(pltpu.with_memory_space_constraint(jnp.asarray(x), pltpu.HBM)
        for x in (links, mat_x, mat_y, decay, factor)))


def exponent(h):
    h2 = -(h[0] + h[1])
    diag = (h[0], h[1], h2)
    re01, im01 = h[3], -h[2]
    re02, im02 = h[5], -h[4]
    re12, im12 = h[7], -h[6]
    n01 = re01 * re01 + im01 * im01
    n02 = re02 * re02 + im02 * im02
    n12 = re12 * re12 + im12 * im12
    s0 = h[0] * h[0] + n01 + n02
    s1 = h[1] * h[1] + n01 + n12
    s2 = h2 * h2 + n02 + n12
    s01re = re02 * re12 + im02 * im12 - h2 * re01
    s01im = im02 * re12 - re02 * im12 - h2 * im01
    s02re = re01 * re12 - im01 * im12 - h[1] * re02
    s02im = re01 * im12 + im01 * re12 - h[1] * im02
    s12re = re01 * re02 + im01 * im02 - h[0] * re12
    s12im = re01 * im02 - im01 * re02 - h[0] * im12
    p = 0.5 * (s0 + s1 + s2)
    cross = (re01 * re12 - im01 * im12) * re02 + (re01 * im12 + im01 * re12) * im02
    d = h[0] * h[1] * h2 + 2.0 * cross - h[0] * n12 - h[1] * n02 - h2 * n01
    pp = p * p
    dd = d * d
    dp = d * p
    cubes = dd + p * pp
    a0 = 1.0 + dd * (p * (2.0 / 40320.0) - 1.0 / 720.0)
    b0 = d * (-1.0 / 6.0 + p * (1.0 / 120.0) - pp * (1.0 / 5040.0))
    a1 = d * (1.0 / 24.0 - p * (2.0 / 720.0) + pp * (3.0 / 40320.0))
    b1 = 1.0 - p * (1.0 / 6.0) + pp * (1.0 / 120.0) - cubes * (1.0 / 5040.0)
    a2 = -0.5 + p * (1.0 / 24.0) - pp * (1.0 / 720.0) + cubes * (1.0 / 40320.0)
    b2 = d * (1.0 / 120.0) - dp * (2.0 / 5040.0)
    re = {}
    im = {}
    for j, s in enumerate((s0, s1, s2)):
        re[j, j] = a0 + a1 * diag[j] + a2 * s
        im[j, j] = b0 + b1 * diag[j] + b2 * s
    for i, j, hr, hi, sr, si in (
        (0, 1, re01, im01, s01re, s01im),
        (0, 2, re02, im02, s02re, s02im),
        (1, 2, re12, im12, s12re, s12im),
    ):
        rr = a1 * hr + a2 * sr
        ii = b1 * hi + b2 * si
        ri = a1 * hi + a2 * si
        ir = b1 * hr + b2 * sr
        re[i, j] = rr - ii
        im[i, j] = ri + ir
        re[j, i] = rr + ii
        im[j, i] = ir - ri
    return [re[i, j] for i in range(3) for j in range(3)] + [
        im[i, j] for i in range(3) for j in range(3)
    ]


def store_kernel(source, out, sem):
    copies = [
        pltpu.make_async_copy(source.at[mu, p], out.at[mu, p], sem.at[mu, p])
        for mu in range(3)
        for p in range(2)
    ]
    for copy in copies:
        copy.start()
    for copy in copies:
        copy.wait()


def store(source):
    return pl.pallas_call(
        store_kernel,
        out_shape=jax.ShapeDtypeStruct(source.shape, F32),
        in_specs=[pl.BlockSpec(memory_space=pltpu.VMEM)],
        out_specs=pl.BlockSpec(memory_space=pl.ANY),
        scratch_shapes=[pltpu.SemaphoreType.DMA((3, 2))],
        compiler_params=pltpu.CompilerParams(vmem_limit_bytes=16 << 20),
        name="store",
    )(source)


def solution(mesh):
    nz, ny = mesh.shape["gz"], mesh.shape["gy"]

    def body(links):
        return store(fix(links, nz, ny))

    spec = P(None, None, None, None, "gz", "gy", None)
    return jax.shard_map(body, mesh=mesh, in_specs=(spec,), out_specs=spec, check_vma=False)
```

time: 48.8 us -> 44.7 us (0.916)
  Pallas kernels: 48.5 us -> 44.6 us
    pallas_call x2, Pallas kernels: 48.5 us -> 44.6 us  [the longest x1 42.8 us: fix(): pl.pallas_call(functools.partial(fix_kernel, nz, ny), out_shape=pltpu.VME...]
where the time goes in v1:
time: 44.7 us; the launch traced here: 44.6 us
  Pallas kernels  44.6 us (100%)
    pallas_call x1, Pallas kernels, fix(): pl.pallas_call(functools.partial(fix_kernel, nz, ny), out_shape=pltpu.VME...  42.8 us
    pallas_call x1, Pallas kernels, store(): pl.pallas_call(store_kernel, out_shape=jax.ShapeDtypeStruct(source.shape,...  1.84 us

profile of v1, /device:TPU:1, one launch (start us, length us, event | category | flops | bytes accessed | tf_op | source)
XLA Modules:
  0.0 44.6 jit_solution(10919046190936632026)
XLA Ops:
  0.0 42.8 %fix.1.source = f32[3,2,3,3,8,16,128]{6,5,4,3,2,1,0:T(8,128)S(1)} custom-call(f32[3,2,3,3,8,16,128]{6,5,4,3,2,1,0:T(8,128)} %links.1, bf16[256,256]{1,0:T(8,128)(2,1)} %constant.8.clone.mat_x_in, bf16[256,256]{1,0:T(8,128)(2,1)} %constant.9.clone.mat_y_in, f32[128,128]{1,0:T(8,128)} %constant.10.clone.decay_in, f32[128,128]{1,0:T(8,128)} %constant.11.clone.factor_in), custom_call_target="tpu_custom_call" | custom-call | tf_op jit(solution)/shard_map/fix/pallas_call | solution.py:568
  42.8 1.8 %store.1 = f32[3,2,3,3,8,16,128]{6,5,4,3,2,1,0:T(8,128)} custom-call(f32[3,2,3,3,8,16,128]{6,5,4,3,2,1,0:T(8,128)S(1)} %fix.1.source), custom_call_target="tpu_custom_call" | custom-call | tf_op jit(solution)/shard_map/store/pallas_call | solution.py:691

commit v2 on v1

v2 whole, which is shorter than its diff:
```python
import functools
import math

import jax
import jax.numpy as jnp
import numpy as np
from jax import lax
from jax.experimental import pallas as pl
from jax.experimental.pallas import tpu as pltpu
from jax.sharding import PartitionSpec as P

L = 128
ALPHA_HALF = 0.04
BZ = 8
BY = 16
NC = 8
MESH = pl.DeviceIdType.MESH
F32 = jnp.float32
BF16 = jnp.bfloat16
HALF = L // 2
NQ = BZ // 2
FORTH = ((0, 2, 4), (0, 0, 2), (1, 2, 4), (1, 0, 2))
BACK = ((0, 0, 2), (1, 0, 2), (0, 2, 3), (1, 2, 3), (0, 3, 4), (1, 3, 4))
STEPS = ((1, 2), (0, 2), (1, 1), (1, 3), (0, 1), (0, 3), (1, 0))


def tables():
    k = np.arange(L)
    angle = 2.0 * np.pi / L * (np.outer(k, k) % L)
    hartley = np.cos(angle) + np.sin(angle)
    high = hartley.astype(np.float32).astype(jnp.bfloat16)
    low = (hartley - high.astype(np.float64)).astype(np.float32).astype(jnp.bfloat16)
    half = np.concatenate([high, low], axis=1)
    mat_x = np.concatenate([half, half], axis=0)
    mat_y = np.ascontiguousarray(mat_x.T)
    momentum = 4.0 * np.sin(np.pi * k / L) ** 2
    mass = momentum[:, None] + momentum[None, :]
    mass[0, 0] = 1.0
    root = np.sqrt(mass * mass / 4.0 + mass)
    decay = 1.0 / (1.0 + mass / 2.0 + root)
    factor = 12.0 * ALPHA_HALF / (L * L) / (2.0 * root)
    decay[0, 0] = 0.0
    factor[0, 0] = 0.0
    paired = [
        np.stack([np.tile(t[:, h * HALF : (h + 1) * HALF], (1, 2)) for h in range(2)])
        for t in (decay, factor)
    ]
    return mat_x, mat_y, paired[0].astype(np.float32), paired[1].astype(np.float32)


def split(x):
    high = x.astype(BF16)
    low = (x - high.astype(F32)).astype(BF16)
    return high, low


def transform_x(planes, mat_x):
    high, low = split(jnp.concatenate(planes, axis=0))
    out = jnp.dot(jnp.concatenate([high, low], axis=1), mat_x, preferred_element_type=F32)
    out = out[:, :L] + out[:, L:]
    return [out[i * L : (i + 1) * L] for i in range(len(planes))]


def transform_y(planes, mat_y):
    high, low = split(jnp.concatenate(planes, axis=1))
    out = jnp.dot(mat_y, jnp.concatenate([high, low], axis=0), preferred_element_type=F32)
    out = out[:L] + out[L:]
    return [out[:, i * L : (i + 1) * L] for i in range(len(planes))]


def algebra(re, im):
    trace_part = (im(0, 0) + im(1, 1) + im(2, 2)) * (1.0 / 3.0)
    return [
        im(0, 0) - trace_part,
        im(1, 1) - trace_part,
        (re(0, 1) - re(1, 0)) * 0.5,
        (im(0, 1) + im(1, 0)) * 0.5,
        (re(0, 2) - re(2, 0)) * 0.5,
        (im(0, 2) + im(2, 0)) * 0.5,
        (re(1, 2) - re(2, 1)) * 0.5,
        (im(1, 2) + im(2, 1)) * 0.5,
    ]


def fix_kernel(
    nz,
    ny,
    links,
    mat_x_in,
    mat_y_in,
    decay_in,
    factor_in,
    out,
    link,
    base,
    send_a,
    edge_y,
    recv_a,
    edge_r,
    edge_z,
    below_z,
    field,
    keep,
    send_b,
    recv_b,
    send_e,
    recv_e,
    send_c,
    recv_c,
    send_d,
    edge_d,
    main,
    smooth,
    above_z,
    edge_g,
    mat_x,
    mat_y,
    decay,
    factor,
    turn,
    turn_edge,
    load_sem,
    small_sem,
    own_sem,
    edge_sem,
    a_send,
    a_recv,
    b_send,
    b_recv,
    c_send,
    c_recv,
    d_send,
    d_recv,
    e_send,
    e_recv,
    z_send,
    z_recv,
    ring,
):
    gz = lax.axis_index("gz")
    gy = lax.axis_index("gy")
    lines = L // nz
    extent = nz * BZ

    side = ny // 2
    half = nz // 2
    my_z, my_y = lax.div(gy, side), lax.rem(gy, side)

    def y_target(r):
        a, b = STEPS[r - 1]
        return lax.rem(my_z + a, 2) * side + lax.rem(my_y + b, side)

    def y_sender(r):
        a, b = STEPS[r - 1]
        return lax.rem(my_z + 2 - a, 2) * side + lax.rem(my_y + side - b, side)

    def z_target(r):
        return lax.rem(gz + r, nz)

    def z_sender(r):
        return lax.rem(gz + nz - r, nz)

    my_half, my_place = lax.div(gz, half), lax.rem(gz, half)

    def near(r):
        return my_half * half + lax.rem(my_place + r, half)

    between = lax.rem(gy + side, ny)

    barrier = pltpu.get_barrier_semaphore()
    for r in range(1, ny):
        pl.semaphore_signal(barrier, inc=1, device_id=(gz, y_target(r)), device_id_type=MESH)
    for device in [z_target(half), z_target(1), z_target(nz - 1)] + [
        near(r) for r in range(1, half)
    ]:
        pl.semaphore_signal(barrier, inc=1, device_id=(device, gy), device_id_type=MESH)

    def load(mu, z):
        return pltpu.make_async_copy(
            links.at[mu, :, :, :, pl.ds(z, 1)],
            link.at[mu, :, :, :, pl.ds(z, 1)],
            load_sem.at[mu, z],
        )

    small = [
        pltpu.make_async_copy(src, dst, small_sem.at[n])
        for n, (src, dst) in enumerate(
            ((mat_x_in, mat_x), (mat_y_in, mat_y), (decay_in, decay), (factor_in, factor))
        )
    ]
    for z in range(BZ):
        load(1, z).start()
    small[0].start()
    load(2, BZ - 1).start()
    load(2, NQ - 1).start()
    for q in range(NQ - 1, -1, -1):
        if q > 0:
            load(2, q + NQ - 1).start()
            load(2, q - 1).start()
        load(0, q + NQ).start()
        load(0, q).start()
    for copy in small[1:]:
        copy.start()

    def remote(src, dst, send, recv, device):
        return pltpu.make_async_remote_copy(
            src_ref=src,
            dst_ref=dst,
            send_sem=send,
            recv_sem=recv,
            device_id=device,
            device_id_type=MESH,
        )

    def rows(block):
        return pl.ds(pl.multiple_of(block * BY, BY), BY)

    def tile(block):
        return pl.ds(pl.multiple_of(block * BZ, BZ), BZ)

    def copy_a(n, r, sender):
        h, lo, hi = FORTH[n]
        return remote(
            send_a.at[h, y_target(r), lo:hi],
            recv_a.at[h, lo:hi, rows(sender)],
            a_send.at[n, r],
            a_recv.at[n, r],
            (gz, y_target(r)),
        )

    def own_a(n):
        h, lo, hi = FORTH[n]
        return pltpu.make_async_copy(
            send_a.at[h, gy, lo:hi], recv_a.at[h, lo:hi, rows(gy)], own_sem.at[0, n]
        )

    def start_a(n):
        for r in range(1, ny):
            copy_a(n, r, gy).start()
        own_a(n).start()

    def copy_edge_a(r, sender):
        return remote(
            edge_y.at[tile(y_target(r))],
            edge_r.at[tile(sender)],
            e_send.at[0, r],
            e_recv.at[0, r],
            (gz, y_target(r)),
        )

    def copy_b(h, r, sender):
        return remote(
            send_b.at[h, z_target(r)],
            recv_b.at[h, sender],
            b_send.at[h, r],
            b_recv.at[h, r],
            (z_target(r), between),
        )

    def copy_e(r, sender):
        return remote(
            send_e.at[0],
            recv_e.at[sender],
            b_send.at[2, r],
            b_recv.at[2, r],
            (z_target(r), gy),
        )

    def copy_c(h, r, sender):
        return remote(
            send_c.at[h, z_target(r)],
            recv_c.at[h, sender],
            c_send.at[h, r],
            c_recv.at[h, r],
            (z_target(r), between),
        )

    def copy_d(n, r, owner):
        h, lo, hi = BACK[n]
        return remote(
            send_d.at[h, lo:hi, rows(y_target(r))],
            main.at[h, owner, lo:hi],
            d_send.at[n, r],
            d_recv.at[n, r],
            (gz, y_target(r)),
        )

    def own_d(n):
        h, lo, hi = BACK[n]
        return pltpu.make_async_copy(
            send_d.at[h, lo:hi, rows(gy)], main.at[h, gy, lo:hi], own_sem.at[1, n]
        )

    def start_d(n):
        for r in range(1, ny):
            copy_d(n, r, gy).start()
        own_d(n).start()

    def copy_edge_d(r, owner):
        return remote(
            edge_d.at[tile(y_target(r))],
            edge_g.at[tile(owner)],
            e_send.at[1, r],
            e_recv.at[1, r],
            (gz, y_target(r)),
        )

    copy_up = remote(edge_z, below_z, z_send.at[0], z_recv.at[0], (z_target(1), gy))
    copy_down = remote(smooth.at[0], above_z, z_send.at[1], z_recv.at[1], (z_target(nz - 1), gy))
    own_edge_a = pltpu.make_async_copy(edge_y.at[tile(gy)], edge_r.at[tile(gy)], edge_sem.at[0])
    own_edge_d = pltpu.make_async_copy(edge_d.at[tile(gy)], edge_g.at[tile(gy)], edge_sem.at[1])

    first_row = lax.broadcasted_iota(jnp.int32, (BY, L), 0) == 0
    left = lax.broadcasted_iota(jnp.int32, (L, L), 1) < HALF
    straight = (lax.broadcasted_iota(jnp.int32, (NC, BZ, L), 2) < HALF) == (
        lax.broadcasted_iota(jnp.int32, (NC, BZ, L), 1) < NQ
    )

    def swap(x):
        return pltpu.roll(x, HALF, 1)

    def pair(x, y):
        return jnp.where(left, x, swap(y)), jnp.where(left, swap(x), y)

    def pair_edge(x):
        other = pltpu.roll(swap(x).reshape(NC, BZ, L), NQ, 1)
        return jnp.where(straight, x.reshape(NC, BZ, L), other).reshape(NC * BZ, L)

    def parts(mu, z):
        return algebra(
            lambda i, j: link[mu, 0, i, j, z], lambda i, j: link[mu, 1, i, j, z]
        )

    def part_y(z, carry):
        load(1, z).wait()
        along = parts(1, z)
        for c in range(NC):
            behind = jnp.where(first_row, 0.0, pltpu.roll(along[c], 1, 0))
            base[c, z] = behind - along[c]
            edge_y[pl.ds(c * BZ + z, 1), :] = along[c][BY - 1 : BY]
        return carry

    lax.fori_loop(0, BZ, part_y, 0)
    load(2, BZ - 1).wait()
    top = parts(2, BZ - 1)
    for c in range(NC):
        edge_z[c] = top[c]
    small[0].wait()

    pl.semaphore_wait(barrier, ny + half + 1)
    copy_up.start()
    for r in range(1, half):
        pl.semaphore_signal(ring.at[0], inc=1, device_id=(near(r), gy), device_id_type=MESH)

    def divergence(z, under, here):
        along = parts(0, z)
        return jnp.concatenate(
            [
                base[c, z] + (pltpu.roll(along[c], 1, 1) - along[c]) + (under[c] - here[c])
                for c in range(NC)
            ],
            axis=0,
        )

    def spread(q, low, high):
        low, high = transform_x([low, high], mat_x[...])
        low, high = pair(low, high)
        send_a[0, :, q] = low.reshape(NC, BY, L)
        send_a[1, :, q] = high.reshape(NC, BY, L)

    def step(t, carry):
        here_low, here_high = carry
        q = NQ - 1 - t
        load(2, q + NQ - 1).wait()
        load(2, q - 1).wait()
        load(0, q + NQ).wait()
        load(0, q).wait()
        under_low = parts(2, q - 1)
        under_high = parts(2, q + NQ - 1)
        spread(
            q, divergence(q, under_low, here_low), divergence(q + NQ, under_high, here_high)
        )
        return under_low, under_high

    load(2, NQ - 1).wait()
    carry = (parts(2, NQ - 1), top)
    carry = lax.fori_loop(0, 2, step, carry)
    start_a(0)
    edge_y[...] = pair_edge(transform_x([edge_y[...]], mat_x[...])[0])
    for r in range(1, ny):
        copy_edge_a(r, gy).start()
    own_edge_a.start()
    carry = lax.fori_loop(2, NQ - 1, step, carry)
    load(0, NQ).wait()
    load(0, 0).wait()
    high = divergence(NQ, parts(2, NQ - 1), carry[1])
    copy_up.wait_recv()
    spread(0, divergence(0, [below_z[c] for c in range(NC)], carry[0]), high)
    for n in range(1, len(FORTH)):
        start_a(n)
    if half > 1:
        pl.semaphore_wait(ring.at[0], half - 1)
    pl.semaphore_signal(
        ring.at[1], inc=1, device_id=(z_target(half), gy), device_id_type=MESH
    )

    for copy in small[1:]:
        copy.wait()
    own_edge_a.wait()
    for r in range(1, ny):
        copy_edge_a(r, y_sender(r)).wait_recv()

    def receive(n):
        h, lo, hi = FORTH[n]
        own_a(n).wait()
        for r in range(1, ny):
            copy_a(n, r, y_sender(r)).wait_recv()
        for q in range(lo, hi):
            edge = pltpu.roll(edge_r[pl.ds(h * NQ + q, ny, stride=BZ), :], 1, 0)
            recv_a[h, q, pl.ds(0, ny, stride=BY), :] += edge
        data = transform_y([recv_a[h, q] for q in range(lo, hi)], mat_y[...])
        for q in range(lo, hi):
            field[h, q] = data[q - lo]

    def power4(x):
        x = x * x
        return x * x

    def moments(h):
        rate = decay[h]
        rate4 = power4(rate)
        up = field[h, 0]
        down = field[h, NQ - 1]
        for q in range(1, NQ):
            up = field[h, q] + rate * up
            down = field[h, NQ - 1 - q] + rate * down
        up = rate * up
        swapped = jnp.where(left, swap(down), swap(up))
        keep[h] = swapped
        send_b[h] = (jnp.where(left, down, up) + rate4 * swapped).reshape(nz, lines, L)
        for r in range(nz):
            copy_b(h, r, gz).start()

    narrow = lax.broadcasted_iota(jnp.int32, (lines, L), 1) < HALF

    def solve(h):
        rate8 = decay[h, pl.ds(pl.multiple_of(gz * lines, lines), lines), :]
        rate8 = power4(rate8 * rate8)
        whole = rate8
        for _ in range(int(math.log2(nz))):
            whole = whole * whole
        images = 1.0 / (1.0 - whole)
        for r in range(nz):
            copy_b(h, r, z_sender(r)).wait_recv()
        mixed = [
            jnp.where(narrow, recv_b[h, nz - 1 - j], recv_b[h, j]) for j in range(nz)
        ]
        state = mixed[0]
        for j in range(1, nz):
            state = mixed[j] + rate8 * state
        state = state * images
        result = []
        for j in range(nz):
            result.append(state)
            state = mixed[j] + rate8 * state
        for j in range(nz):
            send_c[h, j] = jnp.where(narrow, result[nz - 1 - j], result[j])
        for r in range(nz):
            copy_c(h, r, gz).start()

    receive(0)
    receive(1)
    pl.semaphore_wait(ring.at[1], 1)
    moments(0)
    lane = lax.broadcasted_iota(jnp.int32, (1, L), 1)
    packed = jnp.zeros((1, L), F32)
    for q in range(NQ):
        row = field[0, q, 0:1, :]
        packed = jnp.where(lane == q, jnp.sum(jnp.where(lane == 0, row, 0.0)), packed)
        packed = jnp.where(lane == q + NQ, jnp.sum(jnp.where(lane == HALF, row, 0.0)), packed)
    send_e[0] = packed
    for r in range(1, nz):
        copy_e(r, gz).start()
    recv_e[gz] = packed
    receive(2)
    receive(3)
    moments(1)
    solve(0)

    for r in range(1, nz):
        copy_e(r, z_sender(r)).wait_recv()
    sources = recv_e[:, 0, :]
    block = lax.broadcasted_iota(jnp.int32, (nz, L), 0)
    plane = lax.broadcasted_iota(jnp.int32, (nz, L), 1)
    constant = (1.0 + extent * extent - 1.0) / extent
    zero_line = []
    for i in range(BZ):
        gap = BZ * (gz - block) + i - plane
        gap = jnp.where(gap < 0, gap + extent, gap).astype(F32)
        weight = constant - (6.0 / extent) * gap * (extent - gap)
        weight = jnp.where(plane < BZ, weight * (ALPHA_HALF / (L * L)), 0.0)
        zero_line.append(jnp.sum(weight * sources))
    solve(1)

    tile_row = lax.broadcasted_iota(jnp.int32, (8, L), 0)
    tile_lane = lax.broadcasted_iota(jnp.int32, (8, L), 1)

    def evaluate(h):
        rate = decay[h]
        scale = factor[h]
        for r in range(nz):
            copy_c(h, r, z_sender(r)).wait_recv()
        outside = recv_c[h].reshape(L, L)
        inside = power4(rate) * outside + keep[h]
        outside = swap(outside)
        down = rate * jnp.where(left, inside, outside)
        for q in range(NQ - 1, -1, -1):
            recv_a[h, q] = down
            if q > 0:
                down = rate * (down + field[h, q])
        up = jnp.where(left, outside, inside)
        for q in range(NQ):
            up = field[h, q] + (rate * up if q > 0 else up)
            recv_a[h, q] = scale * (up + recv_a[h, q])
            if h == 0:
                low = jnp.where((tile_row == 0) & (tile_lane == 0), zero_line[q], 0.0)
                high = jnp.where(
                    (tile_row == 0) & (tile_lane == HALF), zero_line[q + NQ], 0.0
                )
                recv_a[h, q, 0:8, :] += low + high

    def inverse(h, lo, hi):
        data = transform_y([recv_a[h, q] for q in range(lo, hi)], mat_y[...])
        for q in range(lo, hi):
            send_d[h, q] = data[q - lo]
            edge = send_d[h, q, pl.ds(0, ny, stride=BY), :]
            edge_d[pl.ds(h * NQ + q, ny, stride=BZ), :] = pltpu.roll(edge, ny - 1, 0)

    evaluate(0)
    inverse(0, 0, 2)
    start_d(0)
    inverse(0, 2, 4)
    evaluate(1)
    inverse(1, 0, 2)
    start_d(1)
    inverse(1, 2, 4)
    for r in range(1, ny):
        copy_edge_d(r, gy).start()
    own_edge_d.start()
    for n in range(2, len(BACK)):
        start_d(n)

    for r in range(1, ny):
        for n in range(len(FORTH)):
            copy_a(n, r, gy).wait_send()
        copy_edge_a(r, gy).wait_send()
    for r in range(nz):
        for h in range(2):
            copy_b(h, r, gz).wait_send()
            copy_c(h, r, gz).wait_send()
    for r in range(1, nz):
        copy_e(r, gz).wait_send()
    copy_up.wait_send()

    def fill(plane, value):
        for s in range(0, BY, 8):
            g = exponent([value(c, s) for c in range(NC)])
            for k in range(18):
                turn[plane, k, s : s + 8] = g[k]

    def rotate(z, directions):
        for s in range(0, BY, 8):
            g = [turn[z, k, s : s + 8] for k in range(18)]
            for mu in directions:
                if mu == 0:
                    ahead = [pltpu.roll(x, L - 1, 1) for x in g]
                elif mu == 1:
                    ahead = [turn[z, k, s + 1 : s + 9] for k in range(18)]
                else:
                    ahead = [turn[z + 1, k, s : s + 8] for k in range(18)]
                rotate_link(link, out, mu, z, s, g, ahead)

    def arrive(n):
        own_d(n).wait()
        for r in range(1, ny):
            copy_d(n, r, y_sender(r)).wait_recv()

    def collect(lo, hi):
        planes = []
        for q in range(lo, hi):
            planes += pair(main[0, :, q].reshape(L, L), main[1, :, q].reshape(L, L))
        data = transform_x(planes, mat_x[...])
        for q in range(lo, hi):
            smooth[q] = data[2 * (q - lo)].reshape(NC, BY, L)
            smooth[q + NQ] = data[2 * (q - lo) + 1].reshape(NC, BY, L)

    def fill_plane(z):
        fill(z, lambda c, s: smooth[z, c, s : s + 8])
        for k in range(18):
            turn[z, k, BY : BY + 1] = turn_edge[k, pl.ds(z, 1)]

    def around(t, first):
        z = first + t * NQ
        fill_plane(z)
        rotate(z, (0, 1))
        return first

    def along_z(t, first):
        rotate(first + t * NQ, (2,))
        return first

    arrive(0)
    arrive(1)
    collect(0, 2)
    copy_down.start()
    own_edge_d.wait()
    for r in range(1, ny):
        copy_edge_d(r, y_sender(r)).wait_recv()
    edge_g[...] = transform_x([pair_edge(edge_g[...])], mat_x[...])[0]
    g = exponent([edge_g[c * BZ : (c + 1) * BZ] for c in range(NC)])
    for k in range(18):
        turn_edge[k] = g[k]
    lax.fori_loop(0, 2, around, 0)
    lax.fori_loop(0, 2, around, 1)
    lax.fori_loop(0, 2, along_z, 0)
    arrive(2)
    arrive(3)
    collect(2, 3)
    lax.fori_loop(0, 2, around, 2)
    lax.fori_loop(0, 2, along_z, 1)
    arrive(4)
    arrive(5)
    collect(3, 4)
    lax.fori_loop(0, 2, around, 3)
    lax.fori_loop(0, 2, along_z, 2)
    copy_down.wait_recv()
    fill(BZ, lambda c, s: above_z[c, s : s + 8])
    lax.fori_loop(0, 2, along_z, 3)

    for r in range(1, ny):
        for n in range(len(BACK)):
            copy_d(n, r, gy).wait_send()
        copy_edge_d(r, gy).wait_send()
    copy_down.wait_send()


def rotate_link(link, out, mu, z, s, g, ahead):
    u = [link[mu, p, i, j, z, s : s + 8] for p in range(2) for i in range(3) for j in range(3)]
    for i in range(3):
        left = []
        for k in range(3):
            re = im = None
            for j in range(3):
                ar, ai = g[3 * i + j], g[9 + 3 * i + j]
                br, bi = u[3 * j + k], u[9 + 3 * j + k]
                tr = ar * br - ai * bi
                ti = ar * bi + ai * br
                re = tr if re is None else re + tr
                im = ti if im is None else im + ti
            left.append((re, im))
        for l in range(3):
            re = im = None
            for k in range(3):
                ar, ai = left[k]
                br, bi = ahead[3 * l + k], ahead[9 + 3 * l + k]
                tr = ar * br + ai * bi
                ti = ai * br - ar * bi
                re = tr if re is None else re + tr
                im = ti if im is None else im + ti
            out[mu, 0, i, l, z, s : s + 8] = re
            out[mu, 1, i, l, z, s : s + 8] = im


def fix(links, nz, ny):
    mat_x, mat_y, decay, factor = tables()
    lines = L // nz
    vmem = pltpu.VMEM
    dma = pltpu.SemaphoreType.DMA
    return pl.pallas_call(
        functools.partial(fix_kernel, nz, ny),
        out_shape=pltpu.VMEM(links.shape, F32),
        in_specs=[pl.BlockSpec(memory_space=pltpu.HBM)] * 5,
        out_specs=pl.BlockSpec(memory_space=pltpu.VMEM),
        scratch_shapes=[
            vmem((3, 2, 3, 3, BZ, BY, L), F32),
            vmem((NC, BZ, BY, L), F32),
            vmem((2, NC, NQ, BY, L), F32),
            vmem((NC * BZ, L), F32),
            vmem((2, NQ, L, L), F32),
            vmem((ny * BZ, L), F32),
            vmem((NC, BY, L), F32),
            vmem((NC, BY, L), F32),
            vmem((2, NQ, L, L), F32),
            vmem((2, L, L), F32),
            vmem((2, nz, lines, L), F32),
            vmem((2, nz, lines, L), F32),
            vmem((1, 1, L), F32),
            vmem((nz, 1, L), F32),
            vmem((2, nz, lines, L), F32),
            vmem((2, nz, lines, L), F32),
            vmem((2, NQ, L, L), F32),
            vmem((ny * BZ, L), F32),
            vmem((2, NC, NQ, BY, L), F32),
            vmem((BZ, NC, BY, L), F32),
            vmem((NC, BY, L), F32),
            vmem((NC * BZ, L), F32),
            vmem((2 * L, 2 * L), BF16),
            vmem((2 * L, 2 * L), BF16),
            vmem((2, L, L), F32),
            vmem((2, L, L), F32),
            vmem((BZ + 1, 18, BY + 8, L), F32),
            vmem((18, BZ, L), F32),
            dma((3, BZ)),
            dma((4,)),
            dma((2, len(BACK))),
            dma((2,)),
            dma((len(FORTH), ny)),
            dma((len(FORTH), ny)),
            dma((3, nz)),
            dma((3, nz)),
            dma((2, nz)),
            dma((2, nz)),
            dma((len(BACK), ny)),
            dma((len(BACK), ny)),
            dma((2, ny)),
            dma((2, ny)),
            dma((2,)),
            dma((2,)),
            pltpu.SemaphoreType.REGULAR((2,)),
        ],
        compiler_params=pltpu.CompilerParams(
            collective_id=0, has_side_effects=True, vmem_limit_bytes=32 << 20
        ),
        name="fix",
    )(*(pltpu.with_memory_space_constraint(jnp.asarray(x), pltpu.HBM)
        for x in (links, mat_x, mat_y, decay, factor)))


def exponent(h):
    h2 = -(h[0] + h[1])
    diag = (h[0], h[1], h2)
    re01, im01 = h[3], -h[2]
    re02, im02 = h[5], -h[4]
    re12, im12 = h[7], -h[6]
    n01 = re01 * re01 + im01 * im01
    n02 = re02 * re02 + im02 * im02
    n12 = re12 * re12 + im12 * im12
    s0 = h[0] * h[0] + n01 + n02
    s1 = h[1] * h[1] + n01 + n12
    s2 = h2 * h2 + n02 + n12
    s01re = re02 * re12 + im02 * im12 - h2 * re01
    s01im = im02 * re12 - re02 * im12 - h2 * im01
    s02re = re01 * re12 - im01 * im12 - h[1] * re02
    s02im = re01 * im12 + im01 * re12 - h[1] * im02
    s12re = re01 * re02 + im01 * im02 - h[0] * re12
    s12im = re01 * im02 - im01 * re02 - h[0] * im12
    p = 0.5 * (s0 + s1 + s2)
    cross = (re01 * re12 - im01 * im12) * re02 + (re01 * im12 + im01 * re12) * im02
    d = h[0] * h[1] * h2 + 2.0 * cross - h[0] * n12 - h[1] * n02 - h2 * n01
    pp = p * p
    dd = d * d
    dp = d * p
    cubes = dd + p * pp
    a0 = 1.0 + dd * (p * (2.0 / 40320.0) - 1.0 / 720.0)
    b0 = d * (-1.0 / 6.0 + p * (1.0 / 120.0) - pp * (1.0 / 5040.0))
    a1 = d * (1.0 / 24.0 - p * (2.0 / 720.0) + pp * (3.0 / 40320.0))
    b1 = 1.0 - p * (1.0 / 6.0) + pp * (1.0 / 120.0) - cubes * (1.0 / 5040.0)
    a2 = -0.5 + p * (1.0 / 24.0) - pp * (1.0 / 720.0) + cubes * (1.0 / 40320.0)
    b2 = d * (1.0 / 120.0) - dp * (2.0 / 5040.0)
    re = {}
    im = {}
    for j, s in enumerate((s0, s1, s2)):
        re[j, j] = a0 + a1 * diag[j] + a2 * s
        im[j, j] = b0 + b1 * diag[j] + b2 * s
    for i, j, hr, hi, sr, si in (
        (0, 1, re01, im01, s01re, s01im),
        (0, 2, re02, im02, s02re, s02im),
        (1, 2, re12, im12, s12re, s12im),
    ):
        rr = a1 * hr + a2 * sr
        ii = b1 * hi + b2 * si
        ri = a1 * hi + a2 * si
        ir = b1 * hr + b2 * sr
        re[i, j] = rr - ii
        im[i, j] = ri + ir
        re[j, i] = rr + ii
        im[j, i] = ir - ri
    return [re[i, j] for i in range(3) for j in range(3)] + [
        im[i, j] for i in range(3) for j in range(3)
    ]


def store_kernel(source, out, sem):
    copies = [
        pltpu.make_async_copy(source.at[mu, p], out.at[mu, p], sem.at[mu, p])
        for mu in range(3)
        for p in range(2)
    ]
    for copy in copies:
        copy.start()
    for copy in copies:
        copy.wait()


def store(source):
    return pl.pallas_call(
        store_kernel,
        out_shape=jax.ShapeDtypeStruct(source.shape, F32),
        in_specs=[pl.BlockSpec(memory_space=pltpu.VMEM)],
        out_specs=pl.BlockSpec(memory_space=pl.ANY),
        scratch_shapes=[pltpu.SemaphoreType.DMA((3, 2))],
        compiler_params=pltpu.CompilerParams(vmem_limit_bytes=16 << 20),
        name="store",
    )(source)


def solution(mesh):
    nz, ny = mesh.shape["gz"], mesh.shape["gy"]

    def body(links):
        return store(fix(links, nz, ny))

    spec = P(None, None, None, None, "gz", "gy", None)
    return jax.shard_map(body, mesh=mesh, in_specs=(spec,), out_specs=spec, check_vma=False)
```

time: 44.7 us -> 42.6 us (0.953)
  Pallas kernels: 44.6 us -> 42.5 us
    pallas_call x1, Pallas kernels: 42.8 us -> 40.6 us  [fix(): pl.pallas_call(functools.partial(fix_kernel, nz, ny), out_shape=pltpu.VME...]
where the time goes in v2:
time: 42.6 us; the launch traced here: 42.5 us
  Pallas kernels  42.5 us (100%)
    pallas_call x1, Pallas kernels, fix(): pl.pallas_call(functools.partial(fix_kernel, nz, ny), out_shape=pltpu.VME...  40.6 us
    pallas_call x1, Pallas kernels, store(): pl.pallas_call(store_kernel, out_shape=jax.ShapeDtypeStruct(source.shape,...  1.84 us

profile of v2, /device:TPU:1, one launch (start us, length us, event | category | flops | bytes accessed | tf_op | source)
XLA Modules:
  0.0 42.5 jit_solution(17160594377889109159)
XLA Ops:
  0.0 40.6 %fix.1.source = f32[3,2,3,3,8,16,128]{6,5,4,3,2,1,0:T(8,128)S(1)} custom-call(f32[3,2,3,3,8,16,128]{6,5,4,3,2,1,0:T(8,128)} %links.1, bf16[256,256]{1,0:T(8,128)(2,1)} %constant.8.clone.mat_x_in, bf16[256,256]{1,0:T(8,128)(2,1)} %constant.9.clone.mat_y_in, f32[2,128,128]{2,1,0:T(8,128)} %constant.10.clone.decay_in, f32[2,128,128]{2,1,0:T(8,128)} %constant.11.clone.factor_in), custom_call_target="tpu_custom_call" | custom-call | tf_op jit(solution)/shard_map/fix/pallas_call | solution.py:679
  40.6 1.8 %store.1 = f32[3,2,3,3,8,16,128]{6,5,4,3,2,1,0:T(8,128)} custom-call(f32[3,2,3,3,8,16,128]{6,5,4,3,2,1,0:T(8,128)S(1)} %fix.1.source), custom_call_target="tpu_custom_call" | custom-call | tf_op jit(solution)/shard_map/store/pallas_call | solution.py:806

commit v3 on v2

--- a/solution.py
+++ b/solution.py
@@ -19,8 +19,8 @@
 BF16 = jnp.bfloat16
 HALF = L // 2
 NQ = BZ // 2
-FORTH = ((0, 2, 4), (0, 0, 2), (1, 2, 4), (1, 0, 2))
-BACK = ((0, 0, 2), (1, 0, 2), (0, 2, 3), (1, 2, 3), (0, 3, 4), (1, 3, 4))
+FORTH = ((0, 2, 4), (0, 1, 2), (1, 2, 4), (0, 0, 1), (1, 0, 2))
+BACK = ((0, 0, 2), (1, 0, 1), (1, 1, 2), (0, 2, 3), (1, 2, 3), (0, 3, 4), (1, 3, 4))
 STEPS = ((1, 2), (0, 2), (1, 1), (1, 3), (0, 1), (0, 3), (1, 0))
 
 
@@ -92,6 +92,7 @@
     factor_in,
     out,
     link,
+    turn,
     base,
     send_a,
     edge_y,
@@ -117,12 +118,9 @@
     mat_y,
     decay,
     factor,
-    turn,
     turn_edge,
     load_sem,
     small_sem,
-    own_sem,
-    edge_sem,
     a_send,
     a_recv,
     b_send,
@@ -175,12 +173,18 @@
     ]:
         pl.semaphore_signal(barrier, inc=1, device_id=(device, gy), device_id_type=MESH)
 
-    def load(mu, z):
-        return pltpu.make_async_copy(
+    def load(mu, z, n):
+        pltpu.make_async_copy(
             links.at[mu, :, :, :, pl.ds(z, 1)],
             link.at[mu, :, :, :, pl.ds(z, 1)],
-            load_sem.at[mu, z],
-        )
+            load_sem.at[n],
+        ).start()
+
+    def settle(ref, sem):
+        pltpu.make_async_copy(ref, ref, sem).wait()
+
+    def loaded(n, planes):
+        settle(link.at[0, :, :, :, 0:planes], load_sem.at[n])
 
     small = [
         pltpu.make_async_copy(src, dst, small_sem.at[n])
@@ -189,16 +193,16 @@
         )
     ]
     for z in range(BZ):
-        load(1, z).start()
+        load(1, z, NQ)
     small[0].start()
-    load(2, BZ - 1).start()
-    load(2, NQ - 1).start()
+    load(2, BZ - 1, NQ + 1)
+    load(2, NQ - 1, NQ + 1)
     for q in range(NQ - 1, -1, -1):
         if q > 0:
-            load(2, q + NQ - 1).start()
-            load(2, q - 1).start()
-        load(0, q + NQ).start()
-        load(0, q).start()
+            load(2, q + NQ - 1, q)
+            load(2, q - 1, q)
+        load(0, q + NQ, q)
+        load(0, q, q)
     for copy in small[1:]:
         copy.start()
 
@@ -223,15 +227,15 @@
         return remote(
             send_a.at[h, y_target(r), lo:hi],
             recv_a.at[h, lo:hi, rows(sender)],
-            a_send.at[n, r],
-            a_recv.at[n, r],
+            a_send.at[0],
+            a_recv.at[n],
             (gz, y_target(r)),
         )
 
     def own_a(n):
         h, lo, hi = FORTH[n]
         return pltpu.make_async_copy(
-            send_a.at[h, gy, lo:hi], recv_a.at[h, lo:hi, rows(gy)], own_sem.at[0, n]
+            send_a.at[h, gy, lo:hi], recv_a.at[h, lo:hi, rows(gy)], a_recv.at[n]
         )
 
     def start_a(n):
@@ -243,8 +247,8 @@
         return remote(
             edge_y.at[tile(y_target(r))],
             edge_r.at[tile(sender)],
-            e_send.at[0, r],
-            e_recv.at[0, r],
+            e_send.at[0],
+            e_recv.at[0],
             (gz, y_target(r)),
         )
 
@@ -252,8 +256,8 @@
         return remote(
             send_b.at[h, z_target(r)],
             recv_b.at[h, sender],
-            b_send.at[h, r],
-            b_recv.at[h, r],
+            b_send.at[0],
+            b_recv.at[h],
             (z_target(r), between),
         )
 
@@ -261,8 +265,8 @@
         return remote(
             send_e.at[0],
             recv_e.at[sender],
-            b_send.at[2, r],
-            b_recv.at[2, r],
+            b_send.at[1],
+            b_recv.at[2],
             (z_target(r), gy),
         )
 
@@ -270,8 +274,8 @@
         return remote(
             send_c.at[h, z_target(r)],
             recv_c.at[h, sender],
-            c_send.at[h, r],
-            c_recv.at[h, r],
+            c_send.at[0],
+            c_recv.at[h],
             (z_target(r), between),
         )
 
@@ -280,15 +284,15 @@
         return remote(
             send_d.at[h, lo:hi, rows(y_target(r))],
             main.at[h, owner, lo:hi],
-            d_send.at[n, r],
-            d_recv.at[n, r],
+            d_send.at[0],
+            d_recv.at[n],
             (gz, y_target(r)),
         )
 
     def own_d(n):
         h, lo, hi = BACK[n]
         return pltpu.make_async_copy(
-            send_d.at[h, lo:hi, rows(gy)], main.at[h, gy, lo:hi], own_sem.at[1, n]
+            send_d.at[h, lo:hi, rows(gy)], main.at[h, gy, lo:hi], d_recv.at[n]
         )
 
     def start_d(n):
@@ -300,15 +304,15 @@
         return remote(
             edge_d.at[tile(y_target(r))],
             edge_g.at[tile(owner)],
-            e_send.at[1, r],
-            e_recv.at[1, r],
+            e_send.at[1],
+            e_recv.at[1],
             (gz, y_target(r)),
         )
 
     copy_up = remote(edge_z, below_z, z_send.at[0], z_recv.at[0], (z_target(1), gy))
     copy_down = remote(smooth.at[0], above_z, z_send.at[1], z_recv.at[1], (z_target(nz - 1), gy))
-    own_edge_a = pltpu.make_async_copy(edge_y.at[tile(gy)], edge_r.at[tile(gy)], edge_sem.at[0])
-    own_edge_d = pltpu.make_async_copy(edge_d.at[tile(gy)], edge_g.at[tile(gy)], edge_sem.at[1])
+    own_edge_a = pltpu.make_async_copy(edge_y.at[tile(gy)], edge_r.at[tile(gy)], e_recv.at[0])
+    own_edge_d = pltpu.make_async_copy(edge_d.at[tile(gy)], edge_g.at[tile(gy)], e_recv.at[1])
 
     first_row = lax.broadcasted_iota(jnp.int32, (BY, L), 0) == 0
     left = lax.broadcasted_iota(jnp.int32, (L, L), 1) < HALF
@@ -332,7 +336,6 @@
         )
 
     def part_y(z, carry):
-        load(1, z).wait()
         along = parts(1, z)
         for c in range(NC):
             behind = jnp.where(first_row, 0.0, pltpu.roll(along[c], 1, 0))
@@ -340,13 +343,12 @@
             edge_y[pl.ds(c * BZ + z, 1), :] = along[c][BY - 1 : BY]
         return carry
 
+    loaded(NQ, BZ)
     lax.fori_loop(0, BZ, part_y, 0)
-    load(2, BZ - 1).wait()
+    loaded(NQ + 1, 2)
     top = parts(2, BZ - 1)
     for c in range(NC):
         edge_z[c] = top[c]
-    small[0].wait()
-
     pl.semaphore_wait(barrier, ny + half + 1)
     copy_up.start()
     for r in range(1, half):
@@ -371,10 +373,7 @@
     def step(t, carry):
         here_low, here_high = carry
         q = NQ - 1 - t
-        load(2, q + NQ - 1).wait()
-        load(2, q - 1).wait()
-        load(0, q + NQ).wait()
-        load(0, q).wait()
+        loaded(q, 4)
         under_low = parts(2, q - 1)
         under_high = parts(2, q + NQ - 1)
         spread(
@@ -382,7 +381,7 @@
         )
         return under_low, under_high
 
-    load(2, NQ - 1).wait()
+    small[0].wait()
     carry = (parts(2, NQ - 1), top)
     carry = lax.fori_loop(0, 2, step, carry)
     start_a(0)
@@ -391,13 +390,14 @@
         copy_edge_a(r, gy).start()
     own_edge_a.start()
     carry = lax.fori_loop(2, NQ - 1, step, carry)
-    load(0, NQ).wait()
-    load(0, 0).wait()
+    start_a(1)
+    start_a(2)
+    loaded(0, 2)
     high = divergence(NQ, parts(2, NQ - 1), carry[1])
     copy_up.wait_recv()
     spread(0, divergence(0, [below_z[c] for c in range(NC)], carry[0]), high)
-    for n in range(1, len(FORTH)):
-        start_a(n)
+    start_a(3)
+    start_a(4)
     if half > 1:
         pl.semaphore_wait(ring.at[0], half - 1)
     pl.semaphore_signal(
@@ -406,15 +406,11 @@
 
     for copy in small[1:]:
         copy.wait()
-    own_edge_a.wait()
-    for r in range(1, ny):
-        copy_edge_a(r, y_sender(r)).wait_recv()
+    settle(edge_r, e_recv.at[0])
 
     def receive(n):
         h, lo, hi = FORTH[n]
-        own_a(n).wait()
-        for r in range(1, ny):
-            copy_a(n, r, y_sender(r)).wait_recv()
+        settle(recv_a.at[h, lo:hi], a_recv.at[n])
         for q in range(lo, hi):
             edge = pltpu.roll(edge_r[pl.ds(h * NQ + q, ny, stride=BZ), :], 1, 0)
             recv_a[h, q, pl.ds(0, ny, stride=BY), :] += edge
@@ -450,8 +446,7 @@
         for _ in range(int(math.log2(nz))):
             whole = whole * whole
         images = 1.0 / (1.0 - whole)
-        for r in range(nz):
-            copy_b(h, r, z_sender(r)).wait_recv()
+        settle(recv_b.at[h], b_recv.at[h])
         mixed = [
             jnp.where(narrow, recv_b[h, nz - 1 - j], recv_b[h, j]) for j in range(nz)
         ]
@@ -470,6 +465,8 @@
 
     receive(0)
     receive(1)
+    receive(2)
+    receive(3)
     pl.semaphore_wait(ring.at[1], 1)
     moments(0)
     lane = lax.broadcasted_iota(jnp.int32, (1, L), 1)
@@ -482,13 +479,11 @@
     for r in range(1, nz):
         copy_e(r, gz).start()
     recv_e[gz] = packed
-    receive(2)
-    receive(3)
+    receive(4)
     moments(1)
     solve(0)
 
-    for r in range(1, nz):
-        copy_e(r, z_sender(r)).wait_recv()
+    settle(recv_e.at[0 : nz - 1], b_recv.at[2])
     sources = recv_e[:, 0, :]
     block = lax.broadcasted_iota(jnp.int32, (nz, L), 0)
     plane = lax.broadcasted_iota(jnp.int32, (nz, L), 1)
@@ -508,8 +503,7 @@
     def evaluate(h):
         rate = decay[h]
         scale = factor[h]
-        for r in range(nz):
-            copy_c(h, r, z_sender(r)).wait_recv()
+        settle(recv_c.at[h], c_recv.at[h])
         outside = recv_c[h].reshape(L, L)
         inside = power4(rate) * outside + keep[h]
         outside = swap(outside)
@@ -543,23 +537,19 @@
     evaluate(1)
     inverse(1, 0, 2)
     start_d(1)
+    start_d(2)
     inverse(1, 2, 4)
     for r in range(1, ny):
         copy_edge_d(r, gy).start()
     own_edge_d.start()
-    for n in range(2, len(BACK)):
+    for n in range(3, len(BACK)):
         start_d(n)
 
-    for r in range(1, ny):
-        for n in range(len(FORTH)):
-            copy_a(n, r, gy).wait_send()
-        copy_edge_a(r, gy).wait_send()
-    for r in range(nz):
-        for h in range(2):
-            copy_b(h, r, gz).wait_send()
-            copy_c(h, r, gz).wait_send()
-    for r in range(1, nz):
-        copy_e(r, gz).wait_send()
+    settle(send_a.at[:, 0 : ny - 1], a_send.at[0])
+    settle(edge_y.at[0 : (ny - 1) * BZ], e_send.at[0])
+    settle(send_b, b_send.at[0])
+    settle(send_c, c_send.at[0])
+    settle(recv_e.at[0 : nz - 1], b_send.at[1])
     copy_up.wait_send()
 
     def fill(plane, value):
@@ -569,21 +559,11 @@
                 turn[plane, k, s : s + 8] = g[k]
 
     def rotate(z, directions):
-        for s in range(0, BY, 8):
-            g = [turn[z, k, s : s + 8] for k in range(18)]
-            for mu in directions:
-                if mu == 0:
-                    ahead = [pltpu.roll(x, L - 1, 1) for x in g]
-                elif mu == 1:
-                    ahead = [turn[z, k, s + 1 : s + 9] for k in range(18)]
-                else:
-                    ahead = [turn[z + 1, k, s : s + 8] for k in range(18)]
-                rotate_link(link, out, mu, z, s, g, ahead)
+        rotate_plane(link, turn, out, z, directions)
 
     def arrive(n):
-        own_d(n).wait()
-        for r in range(1, ny):
-            copy_d(n, r, y_sender(r)).wait_recv()
+        h, lo, hi = BACK[n]
+        settle(main.at[h, :, lo:hi], d_recv.at[n])
 
     def collect(lo, hi):
         planes = []
@@ -596,52 +576,67 @@
 
     def fill_plane(z):
         fill(z, lambda c, s: smooth[z, c, s : s + 8])
+
+    def add_edge(z):
         for k in range(18):
             turn[z, k, BY : BY + 1] = turn_edge[k, pl.ds(z, 1)]
-
-    def around(t, first):
-        z = first + t * NQ
-        fill_plane(z)
-        rotate(z, (0, 1))
-        return first
 
     def along_z(t, first):
         rotate(first + t * NQ, (2,))
         return first
 
+    def around(t, first):
+        z = first + t * NQ
+        add_edge(z)
+        rotate(z, (0, 1))
+        return first
+
+    def fill_pair(q):
+        lax.fori_loop(0, 2, lambda t, first: (fill_plane(first + t * NQ), first)[1], q)
+
     arrive(0)
     arrive(1)
-    collect(0, 2)
+    collect(0, 1)
     copy_down.start()
-    own_edge_d.wait()
-    for r in range(1, ny):
-        copy_edge_d(r, y_sender(r)).wait_recv()
+    fill_pair(0)
+    settle(edge_g, e_recv.at[1])
     edge_g[...] = transform_x([pair_edge(edge_g[...])], mat_x[...])[0]
     g = exponent([edge_g[c * BZ : (c + 1) * BZ] for c in range(NC)])
     for k in range(18):
         turn_edge[k] = g[k]
     lax.fori_loop(0, 2, around, 0)
-    lax.fori_loop(0, 2, around, 1)
-    lax.fori_loop(0, 2, along_z, 0)
-    arrive(2)
-    arrive(3)
-    collect(2, 3)
-    lax.fori_loop(0, 2, around, 2)
-    lax.fori_loop(0, 2, along_z, 1)
-    arrive(4)
+    for n, q in ((2, 1), (4, 2)):
+        arrive(n)
+        if q > 1:
+            arrive(n - 1)
+        collect(q, q + 1)
+        fill_pair(q)
+        lax.fori_loop(0, 2, around, q)
+        lax.fori_loop(0, 2, along_z, q - 1)
     arrive(5)
+    arrive(6)
     collect(3, 4)
-    lax.fori_loop(0, 2, around, 3)
-    lax.fori_loop(0, 2, along_z, 2)
+    fill_pair(3)
+    lax.fori_loop(0, 2, lambda t, first: (add_edge(first + t * NQ), first)[1], 3)
     copy_down.wait_recv()
     fill(BZ, lambda c, s: above_z[c, s : s + 8])
-    lax.fori_loop(0, 2, along_z, 3)
-
-    for r in range(1, ny):
-        for n in range(len(BACK)):
-            copy_d(n, r, gy).wait_send()
-        copy_edge_d(r, gy).wait_send()
+
+    settle(send_d.at[:, :, 0 : (ny - 1) * BY], d_send.at[0])
+    settle(edge_d.at[0 : (ny - 1) * BZ], e_send.at[1])
     copy_down.wait_send()
+
+
+def rotate_plane(link, turn, out, z, directions):
+    for s in range(0, BY, 8):
+        g = [turn[z, k, s : s + 8] for k in range(18)]
+        for mu in directions:
+            if mu == 0:
+                ahead = [pltpu.roll(x, L - 1, 1) for x in g]
+            elif mu == 1:
+                ahead = [turn[z, k, s + 1 : s + 9] for k in range(18)]
+            else:
+                ahead = [turn[z + 1, k, s : s + 8] for k in range(18)]
+            rotate_link(link, out, mu, z, s, g, ahead)
 
 
 def rotate_link(link, out, mu, z, s, g, ahead):
@@ -678,11 +673,14 @@
     dma = pltpu.SemaphoreType.DMA
     return pl.pallas_call(
         functools.partial(fix_kernel, nz, ny),
-        out_shape=pltpu.VMEM(links.shape, F32),
+        out_shape=(
+            pltpu.VMEM(links.shape, F32),
+            pltpu.VMEM(links.shape, F32),
+            pltpu.VMEM((BZ + 1, 18, BY + 8, L), F32),
+        ),
         in_specs=[pl.BlockSpec(memory_space=pltpu.HBM)] * 5,
-        out_specs=pl.BlockSpec(memory_space=pltpu.VMEM),
+        out_specs=(pl.BlockSpec(memory_space=pltpu.VMEM),) * 3,
         scratch_shapes=[
-            vmem((3, 2, 3, 3, BZ, BY, L), F32),
             vmem((NC, BZ, BY, L), F32),
             vmem((2, NC, NQ, BY, L), F32),
             vmem((NC * BZ, L), F32),
@@ -708,22 +706,19 @@
             vmem((2 * L, 2 * L), BF16),
             vmem((2, L, L), F32),
             vmem((2, L, L), F32),
-            vmem((BZ + 1, 18, BY + 8, L), F32),
             vmem((18, BZ, L), F32),
-            dma((3, BZ)),
+            dma((NQ + 2,)),
             dma((4,)),
-            dma((2, len(BACK))),
+            dma((1,)),
+            dma((len(FORTH),)),
             dma((2,)),
-            dma((len(FORTH), ny)),
-            dma((len(FORTH), ny)),
-            dma((3, nz)),
-            dma((3, nz)),
-            dma((2, nz)),
-            dma((2, nz)),
-            dma((len(BACK), ny)),
-            dma((len(BACK), ny)),
-            dma((2, ny)),
-            dma((2, ny)),
+            dma((3,)),
+            dma((1,)),
+            dma((2,)),
+            dma((1,)),
+            dma((len(BACK),)),
+            dma((2,)),
+            dma((2,)),
             dma((2,)),
             dma((2,)),
             pltpu.SemaphoreType.REGULAR((2,)),
@@ -790,35 +785,46 @@
     ]
 
 
-def store_kernel(source, out, sem):
-    copies = [
-        pltpu.make_async_copy(source.at[mu, p], out.at[mu, p], sem.at[mu, p])
-        for mu in range(3)
-        for p in range(2)
-    ]
-    for copy in copies:
-        copy.start()
-    for copy in copies:
-        copy.wait()
-
-
-def store(source):
+def store_kernel(source, link, turn, out, last, sem):
+    def put(src, lo, hi, mus):
+        for mu in mus:
+            pltpu.make_async_copy(
+                src.at[mu, :, :, :, lo:hi], out.at[mu, :, :, :, lo:hi], sem.at[0]
+            ).start()
+
+    put(source, 0, 2, (0, 1, 2))
+    put(source, NQ, NQ + 2, (0, 1, 2))
+    put(source, 2, 3, (0, 1))
+    put(source, NQ + 2, NQ + 3, (0, 1))
+    for z in (2, NQ + 2):
+        rotate_plane(link, turn, last, z, (2,))
+        put(last, z, z + 1, (2,))
+    for z in (3, NQ + 3):
+        rotate_plane(link, turn, last, z, (0, 1, 2))
+        put(last, z, z + 1, (0, 1, 2))
+    pltpu.make_async_copy(source, out, sem.at[0]).wait()
+
+
+def store(source, link, turn):
     return pl.pallas_call(
         store_kernel,
         out_shape=jax.ShapeDtypeStruct(source.shape, F32),
-        in_specs=[pl.BlockSpec(memory_space=pltpu.VMEM)],
+        in_specs=[pl.BlockSpec(memory_space=pltpu.VMEM)] * 3,
         out_specs=pl.BlockSpec(memory_space=pl.ANY),
-        scratch_shapes=[pltpu.SemaphoreType.DMA((3, 2))],
+        scratch_shapes=[
+            pltpu.VMEM((3, 2, 3, 3, BZ, BY, L), F32),
+            pltpu.SemaphoreType.DMA((1,)),
+        ],
         compiler_params=pltpu.CompilerParams(vmem_limit_bytes=16 << 20),
         name="store",
-    )(source)
+    )(source, link, turn)
 
 
 def solution(mesh):
     nz, ny = mesh.shape["gz"], mesh.shape["gy"]
 
     def body(links):
-        return store(fix(links, nz, ny))
+        return store(*fix(links, nz, ny))
 
     spec = P(None, None, None, None, "gz", "gy", None)
     return jax.shard_map(body, mesh=mesh, in_specs=(spec,), out_specs=spec, check_vma=False)

time: 42.6 us -> 37.9 us (0.89)
  Pallas kernels: 42.5 us -> 37.7 us
    pallas_call x1, Pallas kernels: 40.6 us -> 35.9 us  [fix(): pl.pallas_call(functools.partial(fix_kernel, nz, ny), out_shape=(pltpu.VM...]
where the time goes in v3:
time: 37.9 us; the launch traced here: 37.7 us
  Pallas kernels  37.7 us (99%)
    pallas_call x1, Pallas kernels, fix(): pl.pallas_call(functools.partial(fix_kernel, nz, ny), out_shape=(pltpu.VM...  35.9 us
    pallas_call x1, Pallas kernels, store(): pl.pallas_call(store_kernel, out_shape=jax.ShapeDtypeStruct(source.shape,...  1.79 us

profile of v3, /device:TPU:1, one launch (start us, length us, event | category | flops | bytes accessed | tf_op | source)
XLA Modules:
  0.0 37.7 jit_solution(7640397734247132886)
XLA Ops:
  0.0 35.9 %fix.1 = (f32[3,2,3,3,8,16,128]{6,5,4,3,2,1,0:T(8,128)S(1)}, f32[3,2,3,3,8,16,128]{6,5,4,3,2,1,0:T(8,128)S(1)}, f32[9,18,24,128]{3,2,1,0:T(8,128)S(1)}) custom-call(f32[3,2,3,3,8,16,128]{6,5,4,3,2,1,0:T(8,128)} %links.1, bf16[256,256]{1,0:T(8,128)(2,1)} %constant.8.clone.mat_x_in, bf16[256,256]{1,0:T(8,128)(2,1)} %constant.9.clone.mat_y_in, ...), custom_call_target="tpu_custom_call" | custom-call | tf_op jit(solution)/shard_map/fix/pallas_call | solution.py:674
  35.9 1.8 %store.1 = f32[3,2,3,3,8,16,128]{6,5,4,3,2,1,0:T(8,128)} custom-call(f32[3,2,3,3,8,16,128]{6,5,4,3,2,1,0:T(8,128)S(1)} %get-tuple-element.8.source, f32[3,2,3,3,8,16,128]{6,5,4,3,2,1,0:T(8,128)S(1)} %get-tuple-element.9.link, f32[9,18,24,128]{3,2,1,0:T(8,128)S(1)} %get-tuple-element.10.turn), custom_call_target="tpu_custom_call" | custom-call | tf_op jit(solution)/shard_map/store/pallas_call | solution.py:809

commit v4 on v3

--- a/solution.py
+++ b/solution.py
@@ -19,8 +19,8 @@
 BF16 = jnp.bfloat16
 HALF = L // 2
 NQ = BZ // 2
-FORTH = ((0, 2, 4), (0, 1, 2), (1, 2, 4), (0, 0, 1), (1, 0, 2))
-BACK = ((0, 0, 2), (1, 0, 1), (1, 1, 2), (0, 2, 3), (1, 2, 3), (0, 3, 4), (1, 3, 4))
+FORTH = ((0, 2, 4), (0, 1, 2), (0, 0, 1), (1, 2, 4), (1, 0, 2))
+BACK = ((0, 0, 2), (0, 2, 3), (1, 0, 1), (1, 1, 2), (1, 2, 3), (0, 3, 4), (1, 3, 4))
 STEPS = ((1, 2), (0, 2), (1, 1), (1, 3), (0, 1), (0, 3), (1, 0))
 
 
@@ -98,8 +98,9 @@
     edge_y,
     recv_a,
     edge_r,
-    edge_z,
-    below_z,
+    face_s,
+    face_r,
+    face,
     field,
     keep,
     send_b,
@@ -168,9 +169,7 @@
     barrier = pltpu.get_barrier_semaphore()
     for r in range(1, ny):
         pl.semaphore_signal(barrier, inc=1, device_id=(gz, y_target(r)), device_id_type=MESH)
-    for device in [z_target(half), z_target(1), z_target(nz - 1)] + [
-        near(r) for r in range(1, half)
-    ]:
+    for device in [z_target(half)] + [near(r) for r in range(1, half)]:
         pl.semaphore_signal(barrier, inc=1, device_id=(device, gy), device_id_type=MESH)
 
     def load(mu, z, n):
@@ -309,7 +308,15 @@
             (gz, y_target(r)),
         )
 
-    copy_up = remote(edge_z, below_z, z_send.at[0], z_recv.at[0], (z_target(1), gy))
+    def copy_face(r, sender):
+        return remote(
+            face_s.at[y_target(r)],
+            face_r.at[rows(sender)],
+            z_send.at[0],
+            z_recv.at[0],
+            (gz, y_target(r)),
+        )
+
     copy_down = remote(smooth.at[0], above_z, z_send.at[1], z_recv.at[1], (z_target(nz - 1), gy))
     own_edge_a = pltpu.make_async_copy(edge_y.at[tile(gy)], edge_r.at[tile(gy)], e_recv.at[0])
     own_edge_d = pltpu.make_async_copy(edge_d.at[tile(gy)], edge_g.at[tile(gy)], e_recv.at[1])
@@ -347,10 +354,12 @@
     lax.fori_loop(0, BZ, part_y, 0)
     loaded(NQ + 1, 2)
     top = parts(2, BZ - 1)
-    for c in range(NC):
-        edge_z[c] = top[c]
-    pl.semaphore_wait(barrier, ny + half + 1)
-    copy_up.start()
+    small[0].wait()
+    face_s[...] = transform_x([jnp.concatenate(top, axis=0)], mat_x[...])[0].reshape(NC, BY, L)
+    pl.semaphore_wait(barrier, ny + half - 1)
+    for r in range(1, ny):
+        copy_face(r, gy).start()
+    pltpu.make_async_copy(face_s.at[gy], face_r.at[rows(gy)], z_recv.at[0]).start()
     for r in range(1, half):
         pl.semaphore_signal(ring.at[0], inc=1, device_id=(near(r), gy), device_id_type=MESH)
 
@@ -358,7 +367,7 @@
         along = parts(0, z)
         return jnp.concatenate(
             [
-                base[c, z] + (pltpu.roll(along[c], 1, 1) - along[c]) + (under[c] - here[c])
+                base[c, z] + (pltpu.roll(along[c], 1, 1) - along[c]) + (-here[c] if under is None else under[c] - here[c])
                 for c in range(NC)
             ],
             axis=0,
@@ -381,21 +390,20 @@
         )
         return under_low, under_high
 
-    small[0].wait()
     carry = (parts(2, NQ - 1), top)
-    carry = lax.fori_loop(0, 2, step, carry)
+    carry = step(0, carry)
+    carry = step(1, carry)
     start_a(0)
     edge_y[...] = pair_edge(transform_x([edge_y[...]], mat_x[...])[0])
     for r in range(1, ny):
         copy_edge_a(r, gy).start()
     own_edge_a.start()
-    carry = lax.fori_loop(2, NQ - 1, step, carry)
+    carry = step(2, carry)
     start_a(1)
-    start_a(2)
     loaded(0, 2)
     high = divergence(NQ, parts(2, NQ - 1), carry[1])
-    copy_up.wait_recv()
-    spread(0, divergence(0, [below_z[c] for c in range(NC)], carry[0]), high)
+    spread(0, divergence(0, None, carry[0]), high)
+    start_a(2)
     start_a(3)
     start_a(4)
     if half > 1:
@@ -433,7 +441,9 @@
         up = rate * up
         swapped = jnp.where(left, swap(down), swap(up))
         keep[h] = swapped
-        send_b[h] = (jnp.where(left, down, up) + rate4 * swapped).reshape(nz, lines, L)
+        beyond = face[h]
+        packed = jnp.where(left, down + rate4 * rate4 * beyond, up + beyond)
+        send_b[h] = (packed + rate4 * swapped).reshape(nz, lines, L)
         for r in range(nz):
             copy_b(h, r, gz).start()
 
@@ -465,8 +475,10 @@
 
     receive(0)
     receive(1)
+    settle(face_r, z_recv.at[0])
+    beyond = transform_y([face_r[...]], mat_y[...])[0]
+    face[0], face[1] = pair(beyond, beyond)
     receive(2)
-    receive(3)
     pl.semaphore_wait(ring.at[1], 1)
     moments(0)
     lane = lax.broadcasted_iota(jnp.int32, (1, L), 1)
@@ -475,10 +487,13 @@
         row = field[0, q, 0:1, :]
         packed = jnp.where(lane == q, jnp.sum(jnp.where(lane == 0, row, 0.0)), packed)
         packed = jnp.where(lane == q + NQ, jnp.sum(jnp.where(lane == HALF, row, 0.0)), packed)
+    row = face[0, 0:1, :]
+    packed = jnp.where(lane == BZ, jnp.sum(jnp.where(lane == 0, row, 0.0)), packed)
     send_e[0] = packed
     for r in range(1, nz):
         copy_e(r, gz).start()
     recv_e[gz] = packed
+    receive(3)
     receive(4)
     moments(1)
     solve(0)
@@ -493,7 +508,7 @@
         gap = BZ * (gz - block) + i - plane
         gap = jnp.where(gap < 0, gap + extent, gap).astype(F32)
         weight = constant - (6.0 / extent) * gap * (extent - gap)
-        weight = jnp.where(plane < BZ, weight * (ALPHA_HALF / (L * L)), 0.0)
+        weight = jnp.where(plane <= BZ, weight * (ALPHA_HALF / (L * L)), 0.0)
         zero_line.append(jnp.sum(weight * sources))
     solve(1)
 
@@ -504,7 +519,7 @@
         rate = decay[h]
         scale = factor[h]
         settle(recv_c.at[h], c_recv.at[h])
-        outside = recv_c[h].reshape(L, L)
+        outside = recv_c[h].reshape(L, L) + jnp.where(left, face[h], 0.0)
         inside = power4(rate) * outside + keep[h]
         outside = swap(outside)
         down = rate * jnp.where(left, inside, outside)
@@ -534,15 +549,16 @@
     inverse(0, 0, 2)
     start_d(0)
     inverse(0, 2, 4)
+    start_d(1)
     evaluate(1)
     inverse(1, 0, 2)
-    start_d(1)
     start_d(2)
+    start_d(3)
     inverse(1, 2, 4)
     for r in range(1, ny):
         copy_edge_d(r, gy).start()
     own_edge_d.start()
-    for n in range(3, len(BACK)):
+    for n in range(4, len(BACK)):
         start_d(n)
 
     settle(send_a.at[:, 0 : ny - 1], a_send.at[0])
@@ -550,7 +566,7 @@
     settle(send_b, b_send.at[0])
     settle(send_c, c_send.at[0])
     settle(recv_e.at[0 : nz - 1], b_send.at[1])
-    copy_up.wait_send()
+    settle(face_s.at[0 : ny - 1], z_send.at[0])
 
     def fill(plane, value):
         for s in range(0, BY, 8):
@@ -585,39 +601,43 @@
         rotate(first + t * NQ, (2,))
         return first
 
-    def around(t, first):
-        z = first + t * NQ
-        add_edge(z)
-        rotate(z, (0, 1))
-        return first
+    def around(q):
+        for z in (q, q + NQ):
+            add_edge(z)
+            rotate(z, (0, 1))
 
     def fill_pair(q):
-        lax.fori_loop(0, 2, lambda t, first: (fill_plane(first + t * NQ), first)[1], q)
+        for z in (q, q + NQ):
+            fill_plane(z)
 
     arrive(0)
-    arrive(1)
+    arrive(2)
     collect(0, 1)
     copy_down.start()
     fill_pair(0)
+    arrive(3)
+    collect(1, 2)
     settle(edge_g, e_recv.at[1])
     edge_g[...] = transform_x([pair_edge(edge_g[...])], mat_x[...])[0]
     g = exponent([edge_g[c * BZ : (c + 1) * BZ] for c in range(NC)])
     for k in range(18):
         turn_edge[k] = g[k]
-    lax.fori_loop(0, 2, around, 0)
-    for n, q in ((2, 1), (4, 2)):
-        arrive(n)
-        if q > 1:
-            arrive(n - 1)
-        collect(q, q + 1)
-        fill_pair(q)
-        lax.fori_loop(0, 2, around, q)
-        lax.fori_loop(0, 2, along_z, q - 1)
+    fill_pair(1)
+    around(0)
+    around(1)
+    lax.fori_loop(0, 2, along_z, 0)
+    arrive(1)
+    arrive(4)
+    collect(2, 3)
+    fill_pair(2)
+    around(2)
+    lax.fori_loop(0, 2, along_z, 1)
     arrive(5)
     arrive(6)
     collect(3, 4)
     fill_pair(3)
-    lax.fori_loop(0, 2, lambda t, first: (add_edge(first + t * NQ), first)[1], 3)
+    for z in (3, 3 + NQ):
+        add_edge(z)
     copy_down.wait_recv()
     fill(BZ, lambda c, s: above_z[c, s : s + 8])
 
@@ -687,7 +707,8 @@
             vmem((2, NQ, L, L), F32),
             vmem((ny * BZ, L), F32),
             vmem((NC, BY, L), F32),
-            vmem((NC, BY, L), F32),
+            vmem((L, L), F32),
+            vmem((2, L, L), F32),
             vmem((2, NQ, L, L), F32),
             vmem((2, L, L), F32),
             vmem((2, nz, lines, L), F32),

time: 37.9 us -> 36.8 us (0.971)
  the two profiles are of different devices: /device:TPU:1 before, /device:TPU:7 now
where the time goes in v4:
time: 36.8 us; the launch traced here: 36.7 us
  Pallas kernels  36.7 us (100%)
    pallas_call x1, Pallas kernels, fix(): pl.pallas_call(functools.partial(fix_kernel, nz, ny), out_shape=(pltpu.VM...  34.9 us
    pallas_call x1, Pallas kernels, store(): pl.pallas_call(store_kernel, out_shape=jax.ShapeDtypeStruct(source.shape,...  1.79 us

profile of v4, /device:TPU:7, one launch (start us, length us, event | category | flops | bytes accessed | tf_op | source)
XLA Modules:
  0.0 36.7 jit_solution(512639407951506083)
XLA Ops:
  0.0 34.9 %fix.1 = (f32[3,2,3,3,8,16,128]{6,5,4,3,2,1,0:T(8,128)S(1)}, f32[3,2,3,3,8,16,128]{6,5,4,3,2,1,0:T(8,128)S(1)}, f32[9,18,24,128]{3,2,1,0:T(8,128)S(1)}) custom-call(f32[3,2,3,3,8,16,128]{6,5,4,3,2,1,0:T(8,128)} %links.1, bf16[256,256]{1,0:T(8,128)(2,1)} %constant.8.clone.mat_x_in, bf16[256,256]{1,0:T(8,128)(2,1)} %constant.9.clone.mat_y_in, ...), custom_call_target="tpu_custom_call" | custom-call | tf_op jit(solution)/shard_map/fix/pallas_call | solution.py:694
  34.9 1.8 %store.1 = f32[3,2,3,3,8,16,128]{6,5,4,3,2,1,0:T(8,128)} custom-call(f32[3,2,3,3,8,16,128]{6,5,4,3,2,1,0:T(8,128)S(1)} %get-tuple-element.8.source, f32[3,2,3,3,8,16,128]{6,5,4,3,2,1,0:T(8,128)S(1)} %get-tuple-element.9.link, f32[9,18,24,128]{3,2,1,0:T(8,128)S(1)} %get-tuple-element.10.turn), custom_call_target="tpu_custom_call" | custom-call | tf_op jit(solution)/shard_map/store/pallas_call | solution.py:830

commit v5 on v4

--- a/solution.py
+++ b/solution.py
@@ -115,6 +115,9 @@
     smooth,
     above_z,
     edge_g,
+    ninth,
+    send_n,
+    above_k,
     mat_x,
     mat_y,
     decay,
@@ -134,6 +137,7 @@
     e_recv,
     z_send,
     z_recv,
+    n_sem,
     ring,
 ):
     gz = lax.axis_index("gz")
@@ -504,7 +508,7 @@
     plane = lax.broadcasted_iota(jnp.int32, (nz, L), 1)
     constant = (1.0 + extent * extent - 1.0) / extent
     zero_line = []
-    for i in range(BZ):
+    for i in range(BZ + 1):
         gap = BZ * (gz - block) + i - plane
         gap = jnp.where(gap < 0, gap + extent, gap).astype(F32)
         weight = constant - (6.0 / extent) * gap * (extent - gap)
@@ -537,6 +541,7 @@
                     (tile_row == 0) & (tile_lane == HALF), zero_line[q + NQ], 0.0
                 )
                 recv_a[h, q, 0:8, :] += low + high
+        ninth[h] = scale * (rate * up + outside)
 
     def inverse(h, lo, hi):
         data = transform_y([recv_a[h, q] for q in range(lo, hi)], mat_y[...])
@@ -561,6 +566,28 @@
     for n in range(4, len(BACK)):
         start_d(n)
 
+    def copy_ninth(r):
+        return remote(
+            send_n.at[rows(y_target(r))],
+            above_k.at[gy],
+            n_sem.at[0],
+            n_sem.at[1],
+            (gz, y_target(r)),
+        )
+
+    @pl.when(my_place == half - 1)
+    def _():
+        plane = jnp.where(left, swap(ninth[0]), ninth[1])
+        origin = (lax.broadcasted_iota(jnp.int32, (L, L), 0) == 0) & (
+            lax.broadcasted_iota(jnp.int32, (L, L), 1) == 0
+        )
+        plane = plane + jnp.where(origin, zero_line[BZ], 0.0)
+        send_n[...] = transform_y([plane], mat_y[...])[0]
+        for r in range(1, ny):
+            copy_ninth(r).start()
+        pltpu.make_async_copy(send_n.at[rows(gy)], above_k.at[gy], n_sem.at[1]).start()
+
+
     settle(send_a.at[:, 0 : ny - 1], a_send.at[0])
     settle(edge_y.at[0 : (ny - 1) * BZ], e_send.at[0])
     settle(send_b, b_send.at[0])
@@ -613,7 +640,10 @@
     arrive(0)
     arrive(2)
     collect(0, 1)
-    copy_down.start()
+    @pl.when(my_place != 0)
+    def _():
+        copy_down.start()
+
     fill_pair(0)
     arrive(3)
     collect(1, 2)
@@ -638,12 +668,27 @@
     fill_pair(3)
     for z in (3, 3 + NQ):
         add_edge(z)
-    copy_down.wait_recv()
+    @pl.when(my_place != half - 1)
+    def _():
+        copy_down.wait_recv()
+
+    @pl.when(my_place == half - 1)
+    def _():
+        settle(above_k, n_sem.at[1])
+        plane = transform_x([above_k[...].reshape(L, L)], mat_x[...])[0]
+        above_z[...] = plane.reshape(NC, BY, L)
+
     fill(BZ, lambda c, s: above_z[c, s : s + 8])
 
     settle(send_d.at[:, :, 0 : (ny - 1) * BY], d_send.at[0])
     settle(edge_d.at[0 : (ny - 1) * BZ], e_send.at[1])
-    copy_down.wait_send()
+    @pl.when(my_place != 0)
+    def _():
+        copy_down.wait_send()
+
+    @pl.when(my_place == half - 1)
+    def _():
+        settle(send_n.at[0 : (ny - 1) * BY], n_sem.at[0])
 
 
 def rotate_plane(link, turn, out, z, directions):
@@ -723,6 +768,9 @@
             vmem((BZ, NC, BY, L), F32),
             vmem((NC, BY, L), F32),
             vmem((NC * BZ, L), F32),
+            vmem((2, L, L), F32),
+            vmem((L, L), F32),
+            vmem((NC, BY, L), F32),
             vmem((2 * L, 2 * L), BF16),
             vmem((2 * L, 2 * L), BF16),
             vmem((2, L, L), F32),
@@ -738,6 +786,7 @@
             dma((2,)),
             dma((1,)),
             dma((len(BACK),)),
+            dma((2,)),
             dma((2,)),
             dma((2,)),
             dma((2,)),

time: 36.8 us -> 35.9 us (0.976)
  the two profiles are of different devices: /device:TPU:7 before, /device:TPU:1 now
where the time goes in v5:
time: 35.9 us; the launch traced here: 35.7 us
  Pallas kernels  35.7 us (99%)
    pallas_call x1, Pallas kernels, fix(): pl.pallas_call(functools.partial(fix_kernel, nz, ny), out_shape=(pltpu.VM...  33.9 us
    pallas_call x1, Pallas kernels, store(): pl.pallas_call(store_kernel, out_shape=jax.ShapeDtypeStruct(source.shape,...  1.79 us

profile of v5, /device:TPU:1, one launch (start us, length us, event | category | flops | bytes accessed | tf_op | source)
XLA Modules:
  0.0 35.7 jit_solution(11467232468756676767)
XLA Ops:
  0.0 33.9 %fix.1 = (f32[3,2,3,3,8,16,128]{6,5,4,3,2,1,0:T(8,128)S(1)}, f32[3,2,3,3,8,16,128]{6,5,4,3,2,1,0:T(8,128)S(1)}, f32[9,18,24,128]{3,2,1,0:T(8,128)S(1)}) custom-call(f32[3,2,3,3,8,16,128]{6,5,4,3,2,1,0:T(8,128)} %links.1, bf16[256,256]{1,0:T(8,128)(2,1)} %constant.8.clone.mat_x_in, bf16[256,256]{1,0:T(8,128)(2,1)} %constant.9.clone.mat_y_in, ...), custom_call_target="tpu_custom_call" | custom-call | tf_op jit(solution)/shard_map/fix/pallas_call | solution.py:739
  33.9 1.8 %store.1 = f32[3,2,3,3,8,16,128]{6,5,4,3,2,1,0:T(8,128)} custom-call(f32[3,2,3,3,8,16,128]{6,5,4,3,2,1,0:T(8,128)S(1)} %get-tuple-element.8.source, f32[3,2,3,3,8,16,128]{6,5,4,3,2,1,0:T(8,128)S(1)} %get-tuple-element.9.link, f32[9,18,24,128]{3,2,1,0:T(8,128)S(1)} %get-tuple-element.10.turn), custom_call_target="tpu_custom_call" | custom-call | tf_op jit(solution)/shard_map/store/pallas_call | solution.py:879

commit v6 on v5

--- a/solution.py
+++ b/solution.py
@@ -19,8 +19,9 @@
 BF16 = jnp.bfloat16
 HALF = L // 2
 NQ = BZ // 2
-FORTH = ((0, 2, 4), (0, 1, 2), (0, 0, 1), (1, 2, 4), (1, 0, 2))
+FORTH = ((0, 3, 4), (0, 2, 3), (0, 1, 2), (0, 0, 1), (1, 2, 4), (1, 0, 2))
 BACK = ((0, 0, 2), (0, 2, 3), (1, 0, 1), (1, 1, 2), (1, 2, 3), (0, 3, 4), (1, 3, 4))
+WAITED = (0, 2, 0, 1, 2, 3, 3)
 STEPS = ((1, 2), (0, 2), (1, 1), (1, 3), (0, 1), (0, 3), (1, 0))
 
 
@@ -288,14 +289,14 @@
             send_d.at[h, lo:hi, rows(y_target(r))],
             main.at[h, owner, lo:hi],
             d_send.at[0],
-            d_recv.at[n],
+            d_recv.at[WAITED[n]],
             (gz, y_target(r)),
         )
 
     def own_d(n):
         h, lo, hi = BACK[n]
         return pltpu.make_async_copy(
-            send_d.at[h, lo:hi, rows(gy)], main.at[h, gy, lo:hi], d_recv.at[n]
+            send_d.at[h, lo:hi, rows(gy)], main.at[h, gy, lo:hi], d_recv.at[WAITED[n]]
         )
 
     def start_d(n):
@@ -396,20 +397,20 @@
 
     carry = (parts(2, NQ - 1), top)
     carry = step(0, carry)
+    start_a(0)
     carry = step(1, carry)
-    start_a(0)
+    start_a(1)
     edge_y[...] = pair_edge(transform_x([edge_y[...]], mat_x[...])[0])
     for r in range(1, ny):
         copy_edge_a(r, gy).start()
     own_edge_a.start()
     carry = step(2, carry)
-    start_a(1)
+    start_a(2)
     loaded(0, 2)
     high = divergence(NQ, parts(2, NQ - 1), carry[1])
     spread(0, divergence(0, None, carry[0]), high)
-    start_a(2)
-    start_a(3)
-    start_a(4)
+    for n in range(3, len(FORTH)):
+        start_a(n)
     if half > 1:
         pl.semaphore_wait(ring.at[0], half - 1)
     pl.semaphore_signal(
@@ -483,6 +484,7 @@
     beyond = transform_y([face_r[...]], mat_y[...])[0]
     face[0], face[1] = pair(beyond, beyond)
     receive(2)
+    receive(3)
     pl.semaphore_wait(ring.at[1], 1)
     moments(0)
     lane = lax.broadcasted_iota(jnp.int32, (1, L), 1)
@@ -497,8 +499,8 @@
     for r in range(1, nz):
         copy_e(r, gz).start()
     recv_e[gz] = packed
-    receive(3)
     receive(4)
+    receive(5)
     moments(1)
     solve(0)
 
@@ -604,9 +606,8 @@
     def rotate(z, directions):
         rotate_plane(link, turn, out, z, directions)
 
-    def arrive(n):
-        h, lo, hi = BACK[n]
-        settle(main.at[h, :, lo:hi], d_recv.at[n])
+    def arrive(n, planes):
+        settle(main.at[0, :, 0:planes], d_recv.at[n])
 
     def collect(lo, hi):
         planes = []
@@ -637,15 +638,14 @@
         for z in (q, q + NQ):
             fill_plane(z)
 
-    arrive(0)
-    arrive(2)
+    arrive(0, 3)
     collect(0, 1)
     @pl.when(my_place != 0)
     def _():
         copy_down.start()
 
     fill_pair(0)
-    arrive(3)
+    arrive(1, 1)
     collect(1, 2)
     settle(edge_g, e_recv.at[1])
     edge_g[...] = transform_x([pair_edge(edge_g[...])], mat_x[...])[0]
@@ -656,14 +656,12 @@
     around(0)
     around(1)
     lax.fori_loop(0, 2, along_z, 0)
-    arrive(1)
-    arrive(4)
+    arrive(2, 2)
     collect(2, 3)
     fill_pair(2)
     around(2)
     lax.fori_loop(0, 2, along_z, 1)
-    arrive(5)
-    arrive(6)
+    arrive(3, 2)
     collect(3, 4)
     fill_pair(3)
     for z in (3, 3 + NQ):
@@ -785,7 +783,7 @@
             dma((1,)),
             dma((2,)),
             dma((1,)),
-            dma((len(BACK),)),
+            dma((4,)),
             dma((2,)),
             dma((2,)),
             dma((2,)),

time: 35.9 us -> 35.9 us (level)
  no operation moved by 1% of the time
where the time goes in v6:
time: 35.9 us; the launch traced here: 35.8 us
  Pallas kernels  35.8 us (100%)
    pallas_call x1, Pallas kernels, fix(): pl.pallas_call(functools.partial(fix_kernel, nz, ny), out_shape=(pltpu.VM...  34 us
    pallas_call x1, Pallas kernels, store(): pl.pallas_call(store_kernel, out_shape=jax.ShapeDtypeStruct(source.shape,...  1.79 us

profile of v6, /device:TPU:1, one launch (start us, length us, event | category | flops | bytes accessed | tf_op | source)
XLA Modules:
  0.0 35.8 jit_solution(4323173282649078766)
XLA Ops:
  0.0 34.0 %fix.1 = (f32[3,2,3,3,8,16,128]{6,5,4,3,2,1,0:T(8,128)S(1)}, f32[3,2,3,3,8,16,128]{6,5,4,3,2,1,0:T(8,128)S(1)}, f32[9,18,24,128]{3,2,1,0:T(8,128)S(1)}) custom-call(f32[3,2,3,3,8,16,128]{6,5,4,3,2,1,0:T(8,128)} %links.1, bf16[256,256]{1,0:T(8,128)(2,1)} %constant.8.clone.mat_x_in, bf16[256,256]{1,0:T(8,128)(2,1)} %constant.9.clone.mat_y_in, ...), custom_call_target="tpu_custom_call" | custom-call | tf_op jit(solution)/shard_map/fix/pallas_call | solution.py:737
  34.0 1.8 %store.1 = f32[3,2,3,3,8,16,128]{6,5,4,3,2,1,0:T(8,128)} custom-call(f32[3,2,3,3,8,16,128]{6,5,4,3,2,1,0:T(8,128)S(1)} %get-tuple-element.8.source, f32[3,2,3,3,8,16,128]{6,5,4,3,2,1,0:T(8,128)S(1)} %get-tuple-element.9.link, f32[9,18,24,128]{3,2,1,0:T(8,128)S(1)} %get-tuple-element.10.turn), custom_call_target="tpu_custom_call" | custom-call | tf_op jit(solution)/shard_map/store/pallas_call | solution.py:877
